TPU v7x, 256 devices: a whole 4x4x8 slice. The times are simulated.
256 devices in a mesh: wide: 32 (over x, z), narrow: 8 (over y, core).
Axes of the slice: x: 4, y: 4, z: 8, core: 2. Of those that a mesh axis runs over, the one named last changes fastest.
Arguments:
- coefficients: bfloat16 [4096, 2, 512], P(('wide', 'narrow')), may hold values from -6 to 6
- radiation: bfloat16 [2, 512, 882], replicated, may hold values from -0.1875 to 0.1875
- interpolation: bfloat16 [882, 3328], replicated, may hold values from -0.21875 to 0.21875
- angles: float32 [8, 3328], replicated, may hold values from -3.140625 to 3.140625
- translations: float32 [316, 2, 3328], P(None, None, 'wide'), may hold values from -0.031746034 to 0.031746034
- sources: int32 [512, 189], P(('wide', 'narrow')), may hold values from 0 to 511
- operators: int32 [512, 189], P(('wide', 'narrow')), may hold values from 0 to 315
- counts: int32 [512], P(('wide', 'narrow')), may hold values from 63 to 189, as said below
Outputs:
- product: float32 [4096, 2, 512], P(('wide', 'narrow'))
Inputs may be any that keep to these rules, and one draw needn't show every extreme that they name: `counts`: entries of a list past its count are not used; some parent has exactly 189 entries and some exactly 63. `sources`: index values; a program may hold and send them packed several to one 32-bit word, as an allowed encoding. `operators`: index values; a program may hold and send them packed several to one 32-bit word, as an allowed encoding.
All inputs are finite; a program needn't handle non-finite values.
Results may differ from a plain program's by a relative error of at most 0.005.
Values sent between devices are 32-bit elements; how exact they have to be, the bound alone decides.
A program may use at most 128 MiB of HBM per device.

v0:
```python
import jax
import jax.numpy as jnp
from jax import lax
from jax.sharding import Mesh
from jax.sharding import PartitionSpec as P

WIDE = ("wide_0", "wide_1")
WIDE_NARROW = ("wide_0", "wide_1", "narrow")


def in_one_piece(arrays, axis, dim, along):
    columns = [a.reshape(*a.shape[:along], -1) for a in arrays]
    both = jnp.concatenate(columns, axis=along)
    whole, at, finished = (lax.all_gather(both, axis, axis=dim, tiled=True), 0, [])
    for a, column in zip(arrays, columns):
        share = whole[..., at : at + column.shape[along]]
        finished.append(share.reshape(*share.shape[:along], *a.shape[along:]))
        at += column.shape[along]
    return tuple(finished)


def in_blocks(value, dim, length):
    before, after = (value.shape[:dim], value.shape[dim + 1 :])
    return jnp.moveaxis(value.reshape(*before, length, -1, *after), dim, 0)


def laid_out(tiles, dim):
    tiles = jnp.moveaxis(tiles, 0, dim)
    shape = tiles.shape
    return tiles.reshape(*shape[:dim], shape[dim] * shape[dim + 1], *shape[dim + 2 :])


def turned_blocks(tiles, axes, turns):
    shape = [lax.axis_size(a) for a in axes]
    tiles = tiles.reshape(*shape, *tiles.shape[1:])
    for k in turns:
        tiles = lax.all_to_all(tiles, axes[k], split_axis=k, concat_axis=k, tiled=True)
    return tiles.reshape(-1, *tiles.shape[len(axes) :])


def stepwise_exchange(value, axes, turns, split_dim, concat_dim):
    tiles = in_blocks(value, split_dim, lax.axis_size(axes))
    return laid_out(turned_blocks(tiles, axes, turns), concat_dim)


def copy_for_each(value, axis):
    copies = jnp.broadcast_to(value, (lax.axis_size(axis), *value.shape))
    return lax.all_to_all(copies, axis, split_axis=0, concat_axis=0, tiled=True)


def gather_directly(value, axis, dim):
    return laid_out(copy_for_each(value, axis), dim)


def product_of(left, right):
    return jnp.dot(left, right, preferred_element_type=jnp.float32)


def translate(patterns, operator_table, source_index, operator_index, weights):
    pat_real = patterns[:, 0]
    pat_imag = patterns[:, 1]
    tab_real = operator_table[:, 0]
    tab_imag = operator_table[:, 1]
    pick_real = jnp.take(pat_real, source_index, axis=0)
    pick_imag = jnp.take(pat_imag, source_index, axis=0)
    oper_real = jnp.take(tab_real, operator_index, axis=0)
    oper_imag = jnp.take(tab_imag, operator_index, axis=0)
    weight = weights[:, :, None]
    total_real = jnp.sum(weight * (oper_real * pick_real - oper_imag * pick_imag), 1)
    total_imag = jnp.sum(weight * (oper_real * pick_imag + oper_imag * pick_real), 1)
    return jnp.stack([total_real, total_imag], 1)


def on_device(
    coefficients, radiation, interpolation, angles, translations, sources, operators, counts
):
    box_dev = coefficients.shape[0]
    parents_dev = box_dev // 8
    leaf_dirs = interpolation.shape[0]
    parent_dirs = interpolation.shape[1]
    n_wide = lax.axis_size(WIDE)
    n_narrow = lax.axis_size("narrow")
    coef_real = coefficients[:, 0]
    coef_imag = coefficients[:, 1]
    rad_real = radiation[0]
    rad_imag = radiation[1]
    leaf_real = product_of(coef_real, rad_real) - product_of(coef_imag, rad_imag)
    leaf_imag = product_of(coef_real, rad_imag) + product_of(coef_imag, rad_real)
    leaf = jnp.stack([leaf_real, leaf_imag], 1).astype(jnp.bfloat16)
    upward = product_of(leaf.reshape(box_dev * 2, leaf_dirs), interpolation).reshape(
        parents_dev, 8, 2, parent_dirs
    )
    cosines = jnp.cos(angles)[None]
    sines = jnp.sin(angles)[None]
    out_real = jnp.sum(cosines * upward[:, :, 0] - sines * upward[:, :, 1], 1)
    out_imag = jnp.sum(cosines * upward[:, :, 1] + sines * upward[:, :, 0], 1)
    outgoing = jnp.stack([out_real, out_imag], 1)
    list_ids, list_ops, list_lens = in_one_piece((sources, operators, counts), WIDE, 0, 1)
    positions = jnp.arange(list_ids.shape[1], dtype=jnp.int32)
    weights = (positions[None, :] < list_lens[:, None]).astype(jnp.float32)
    own_slice = stepwise_exchange(outgoing, WIDE, (0, 1), 2, 0)
    every = gather_directly(own_slice, "narrow", 0)
    owner = list_ids // parents_dev
    local_ids = (
        owner % n_narrow * n_wide + owner // n_narrow
    ) * parents_dev + list_ids % parents_dev
    incoming = translate(every, translations, local_ids, list_ops, weights)
    back = lax.all_to_all(incoming, WIDE, split_axis=0, concat_axis=2, tiled=True)
    in_real = back[:, 0]
    in_imag = back[:, 1]
    down_real = cosines * in_real[:, None] + sines * in_imag[:, None]
    down_imag = cosines * in_imag[:, None] - sines * in_real[:, None]
    downward = jnp.stack([down_real, down_imag], 2).astype(jnp.bfloat16)
    received = lax.dot_general(
        downward.reshape(box_dev * 2, parent_dirs),
        interpolation,
        (((1,), (1,)), ((), ())),
        preferred_element_type=jnp.float32,
    )
    received = received.astype(jnp.bfloat16).reshape(box_dev, 2, leaf_dirs)
    dims = (((1,), (1,)), ((), ()))
    recv_real = received[:, 0]
    recv_imag = received[:, 1]
    res_real = lax.dot_general(
        recv_real, rad_real, dims, preferred_element_type=jnp.float32
    ) + lax.dot_general(recv_imag, rad_imag, dims, preferred_element_type=jnp.float32)
    res_imag = lax.dot_general(
        recv_imag, rad_real, dims, preferred_element_type=jnp.float32
    ) - lax.dot_general(recv_real, rad_imag, dims, preferred_element_type=jnp.float32)
    return jnp.stack([res_real, res_imag], 1)


def solution(mesh):
    split = Mesh(mesh.devices.reshape(4, 8, mesh.shape["narrow"]), ("wide_0", "wide_1", "narrow"))
    placed = (
        P(WIDE_NARROW, None, None),
        P(),
        P(),
        P(),
        P(None, None, WIDE),
        P(WIDE_NARROW, None),
        P(WIDE_NARROW, None),
        P(WIDE_NARROW),
    )
    return jax.shard_map(
        on_device,
        mesh=split,
        in_specs=placed,
        out_specs=P(WIDE_NARROW, None, None),
        check_vma=False,
    )
```

profile of v0, /device:TPU:1, one launch (start us, length us, event | category | flops | bytes accessed | tf_op | source)
XLA Modules:
  0.0 266.4 jit_solution(17825254175457478117)
XLA Ops:
  0.0 0.9 fusion.32
  0.9 1.3 fusion.29
  2.2 0.0 slice-start
  2.2 5.3 %fusion.27 = (bf16[1,512,882]{1,0,2:T(2,128)(2,1)S(1)}, bf16[1,512,882]{1,0,2:T(2,128)(2,1)S(1)}) fusion(bf16[2,512,882]{1,0,2:T(2,128)(2,1)} %param.13), kind=kLoop, calls=%fused_computation.78 | loop fusion | bytes 3612672 | tf_op jit(solution)/shard_map/slice | solution.py:86
  7.4 0.0 slice-start.1
  7.5 0.5 copy_bitcast_fusion
  8.0 0.0 copy-start.3
  8.0 0.0 copy-start.1
  8.0 0.0 copy-start.2
  8.0 0.3 fusion.24
  8.4 0.4 fusion.25
  8.7 0.4 fusion.6
  9.1 0.4 fusion.7
  9.4 0.2 slice-done.1
  9.6 0.9 fusion
  10.6 0.2 subtract_reduce_fusion
  10.8 0.1 stack.45
  10.9 0.1 stack.46
  11.0 0.7 copy.66
  11.7 4.8 %all-to-all-start = ((f32[4,8,2,2,104]{4,2,1,3,0:T(2,128)}), f32[4,8,2,2,104]{4,2,1,3,0:T(2,128)S(1)}, u32[]{:S(2)}, u32[]{:S(2)}) async-start(f32[4,8,2,2,104]{4,2,1,3,0:T(2,128)} %copy.66), calls=%async_computation | async-start | bytes 131072 | tf_op jit(solution)/shard_map/all_to_all | solution.py:37
  16.5 0.1 copy.55
  16.6 0.1 add_bitcast_fusion
  16.7 36.8 %all-gather = s32[32,2,379]{2,1,0:T(2,128)S(1)} all-gather(s32[1,2,379]{2,1,0:T(2,128)S(1)} %add_bitcast_fusion), channel_id=1, replica_groups=mesh['wide_0'=4,'wide_1'=8,'narrow'=8] {'wide_0','wide_1'}, dimensions={0}, use_global_device_ids=true | all-gather | bytes 100056 | tf_op jit(solution)/shard_map/all_gather | solution.py:14
  53.5 0.1 reshape.129
  53.5 0.1 slice.81
  53.6 0.1 copy.87
  53.7 0.2 compare_and_fusion
  53.9 0.7 copy.67
  54.6 4.2 %all-to-all-start.1 = ((f32[4,8,2,2,104]{4,2,0,3,1:T(2,128)}), f32[4,8,2,2,104]{4,2,0,3,1:T(2,128)S(1)}, u32[]{:S(2)}, u32[]{:S(2)}) async-start(f32[4,8,2,2,104]{4,2,0,3,1:T(2,128)} %copy.67), calls=%async_computation.1 | async-start | bytes 131072 | tf_op jit(solution)/shard_map/all_to_all | solution.py:37
  58.8 0.1 compare_select_fusion.1
  58.9 0.2 reshape.130
  59.1 0.2 reshape.134
  59.3 0.1 copy.88
  59.4 0.1 copy.94
  59.5 6.5 %all-to-all-done.1 = f32[4,8,2,2,104]{4,2,0,3,1:T(2,128)S(1)} async-done(((f32[4,8,2,2,104]{4,2,0,3,1:T(2,128)}), f32[4,8,2,2,104]{4,2,0,3,1:T(2,128)S(1)}, u32[]{:S(2)}, u32[]{:S(2)}) %all-to-all-start.1) | async-done | bytes 53280 | tf_op jit(solution)/shard_map/all_to_all | solution.py:37
  66.0 0.9 broadcast_in_dim.25
  66.9 17.2 %all-to-all-start.2 = ((f32[8,64,2,104]{3,1,2,0:T(8,128)}), f32[8,64,2,104]{3,1,2,0:T(8,128)S(1)}, u32[]{:S(2)}, u32[]{:S(2)}) async-start(f32[8,64,2,104]{3,1,2,0:T(8,128)} %broadcast_in_dim.25), calls=%async_computation.2 | async-start | bytes 1048576 | tf_op jit(solution)/shard_map/all_to_all | solution.py:48
  84.1 23.4 %gather_fusion.2 = f32[12096,104]{1,0:T(8,128)} fusion(f32[316,104]{1,0:T(8,128)S(1)} %bitcast.91, s32[12288]{0:T(1024)S(1)} %pad_clamp_fusion.1), kind=kCustom, calls=%fused_computation.2.clone | custom fusion | bytes 10112256 | tf_op jit(solution)/shard_map/jit(_take)/gather | solution.py:67
  107.5 6.0 %reshape.149 = f32[64,189,104]{2,1,0:T(8,128)} reshape(f32[12096,104]{1,0:T(8,128)} %gather_fusion.2) | data formatting | bytes 10063872 | tf_op jit(solution)/shard_map/jit(_take)/gather | solution.py:67
  113.5 8.6 %copy.83 = f32[64,189,104]{1,0,2:T(8,128)} copy(f32[64,189,104]{2,1,0:T(8,128)} %reshape.149) | data formatting | bytes 10063872 | tf_op jit(solution)/shard_map/jit(_take)/gather | solution.py:67
  122.1 23.3 %gather_fusion = f32[12096,104]{1,0:T(8,128)} fusion(f32[316,104]{1,0:T(8,128)S(1)} %bitcast.90, s32[12288]{0:T(1024)S(1)} %pad_clamp_fusion.1), kind=kCustom, calls=%fused_computation.clone | custom fusion | bytes 10112256 | tf_op jit(solution)/shard_map/jit(_take)/gather | solution.py:66
  145.4 5.9 %reshape.147 = f32[64,189,104]{2,1,0:T(8,128)} reshape(f32[12096,104]{1,0:T(8,128)} %gather_fusion) | data formatting | bytes 10063872 | tf_op jit(solution)/shard_map/jit(_take)/gather | solution.py:66
  151.3 8.6 %copy.81 = f32[64,189,104]{1,0,2:T(8,128)} copy(f32[64,189,104]{2,1,0:T(8,128)} %reshape.147) | data formatting | bytes 10063872 | tf_op jit(solution)/shard_map/jit(_take)/gather | solution.py:66
  160.1 23.4 %gather_fusion.1 = f32[12096,104]{1,0:T(8,128)} fusion(f32[512,104]{1,0:T(8,128)S(1)} %get-tuple-element.15, s32[12288]{0:T(1024)S(1)} %pad_clamp_fusion), kind=kCustom, calls=%fused_computation.1.clone | custom fusion | bytes 10112256 | tf_op jit(solution)/shard_map/jit(_take)/gather | solution.py:64
  183.4 5.9 %reshape.148 = f32[64,189,104]{2,1,0:T(8,128)} reshape(f32[12096,104]{1,0:T(8,128)} %gather_fusion.1) | data formatting | bytes 10063872 | tf_op jit(solution)/shard_map/jit(_take)/gather | solution.py:64
  189.4 8.6 %copy.82 = f32[64,189,104]{1,0,2:T(8,128)} copy(f32[64,189,104]{2,1,0:T(8,128)} %reshape.148) | data formatting | bytes 10063872 | tf_op jit(solution)/shard_map/jit(_take)/gather | solution.py:64
  198.0 23.3 %gather_fusion.3 = f32[12096,104]{1,0:T(8,128)} fusion(f32[512,104]{1,0:T(8,128)S(1)} %get-tuple-element.16, s32[12288]{0:T(1024)S(1)} %pad_clamp_fusion), kind=kCustom, calls=%fused_computation.3.clone | custom fusion | bytes 10112256 | tf_op jit(solution)/shard_map/jit(_take)/gather | solution.py:65
  221.3 5.9 %reshape.150 = f32[64,189,104]{2,1,0:T(8,128)} reshape(f32[12096,104]{1,0:T(8,128)} %gather_fusion.3) | data formatting | bytes 10063872 | tf_op jit(solution)/shard_map/jit(_take)/gather | solution.py:65
  227.2 8.6 %copy.84 = f32[64,189,104]{1,0,2:T(8,128)} copy(f32[64,189,104]{2,1,0:T(8,128)} %reshape.150) | data formatting | bytes 10063872 | tf_op jit(solution)/shard_map/jit(_take)/gather | solution.py:65
  235.8 11.1 %multiply_reduce_fusion.1 = (f32[64,104]{0,1:T(8,128)S(1)}, f32[64,104]{0,1:T(8,128)S(1)}) fusion(f32[64,189,104]{1,0,2:T(8,128)} %copy.84, f32[64,189,104]{1,0,2:T(8,128)} %copy.83, f32[64,189,104]{1,0,2:T(8,128)} %copy.82, f32[64,189,104]{1,0,2:T(8,128)} %copy.81, f32[64,189]{1,0:T(8,128)S(1)} %get-tuple-element.32, ...), kind=kLoop, calls=%fused_computation.5 | loop fusion | flops 17598464 | bytes 20253568 | tf_op jit(solution)/shard_map/reduce_sum | solution.py:69
  247.0 0.1 copy.74
  247.1 11.8 %all_to_all.33 = f32[64,2,104]{2,1,0:T(2,128)S(1)} all-to-all(f32[64,2,104]{2,1,0:T(2,128)S(1)} %copy.74), channel_id=1, replica_groups=mesh['wide_0'=4,'wide_1'=8,'narrow'=8] {'wide_0','wide_1'}, dimensions={0} | all-to-all | bytes 106496 | tf_op jit(solution)/shard_map/all_to_all | solution.py:108
  258.9 0.1 all_to_all.28
  259.1 0.4 add_convert_fusion
  259.6 0.5 pad_maximum_fusion
  260.1 0.1 convert_element_type.19
  260.2 4.5 %convolution_convert_fusion = bf16[32,882]{1,0:T(8,128)(2,1)S(1)} fusion(bf16[32,3328]{1,0:T(8,128)(2,1)S(1)} %convert_element_type.19, bf16[882,3328]{1,0:T(8,128)(2,1)} %param.14), kind=kOutput, calls=%fused_computation.8 | convolution fusion | flops 187887168 | bytes 6140032 | tf_op jit(solution)/shard_map/dot_general | solution.py:114
  264.6 0.1 reshape.87
  264.7 0.1 fusion.30
  264.8 0.2 fusion.22
  265.0 0.2 fusion.23
  265.3 0.2 fusion.5
  265.5 0.2 fusion.4
  265.7 0.7 copy.79
  (23 shorter events, 0.3 us)
Async XLA Ops:
  2.2 7.3 %slice-start = ((s8[5910528]{0:T(1024)(128)(4,1)}), s8[1716224]{0:T(1024)(128)(4,1)S(1)}, s32[]{:S(2)}) async-start(s8[5910528]{0:T(1024)(128)(4,1)} %bitcast.92), calls=%async_computation.4 | async-start | bytes 3432448
  7.4 2.2 slice-start.1
  8.0 8.5 %copy-start.3 = (s32[2]{0:T(128)S(1)}, s32[2]{0:T(128)}, u32[]{:S(2)}) copy-start(s32[2]{0:T(128)} %param.19) | copy-start | bytes 28
  8.0 8.6 %copy-start.1 = (s32[2,189]{1,0:T(2,128)S(1)}, s32[2,189]{1,0:T(2,128)}, u32[]{:S(2)}) copy-start(s32[2,189]{1,0:T(2,128)} %param.18) | copy-start | bytes 4540
  8.0 8.6 %copy-start.2 = (s32[2,189]{1,0:T(2,128)S(1)}, s32[2,189]{1,0:T(2,128)}, u32[]{:S(2)}) copy-start(s32[2,189]{1,0:T(2,128)} %param.17) | copy-start | bytes 4540
  8.0 45.7 %copy-start = (f32[316,2,104]{0,2,1:T(8,128)S(1)}, f32[316,2,104]{0,2,1:T(8,128)}, u32[]{:S(2)}) copy-start(f32[316,2,104]{0,2,1:T(8,128)} %param.16) | copy-start | bytes 788740
  11.7 42.2 %all-to-all-start = ((f32[4,8,2,2,104]{4,2,1,3,0:T(2,128)}), f32[4,8,2,2,104]{4,2,1,3,0:T(2,128)S(1)}, u32[]{:S(2)}, u32[]{:S(2)}) async-start(f32[4,8,2,2,104]{4,2,1,3,0:T(2,128)} %copy.66), calls=%async_computation | async-start | bytes 131072 | tf_op jit(solution)/shard_map/all_to_all | solution.py:37
  54.6 11.4 %all-to-all-start.1 = ((f32[4,8,2,2,104]{4,2,0,3,1:T(2,128)}), f32[4,8,2,2,104]{4,2,0,3,1:T(2,128)S(1)}, u32[]{:S(2)}, u32[]{:S(2)}) async-start(f32[4,8,2,2,104]{4,2,0,3,1:T(2,128)} %copy.67), calls=%async_computation.1 | async-start | bytes 131072 | tf_op jit(solution)/shard_map/all_to_all | solution.py:37
  66.9 93.1 %all-to-all-start.2 = ((f32[8,64,2,104]{3,1,2,0:T(8,128)}), f32[8,64,2,104]{3,1,2,0:T(8,128)S(1)}, u32[]{:S(2)}, u32[]{:S(2)}) async-start(f32[8,64,2,104]{3,1,2,0:T(8,128)} %broadcast_in_dim.25), calls=%async_computation.2 | async-start | bytes 1048576 | tf_op jit(solution)/shard_map/all_to_all | solution.py:48
where the time goes:
time: 268 us; the launch traced here: 266 us
  local copies, waits for them, and re-layouts  164 us (61%)
  blocking collectives  48.6 us (18%)
  starting transfers between devices  26.2 us (10%)
  other arithmetic  12.6 us (5%)
  matrix products  7.72 us (3%)
  waiting for transfers between devices  6.51 us (2%)
    gather x3, local copies, waits for them, and re-layouts, translate(): oper_imag = jnp.take(tab_imag, operator_index, axis=0)  38 us
    gather x3, local copies, waits for them, and re-layouts, translate(): pick_real = jnp.take(pat_real, source_index, axis=0)  37.9 us
    gather x3, local copies, waits for them, and re-layouts, translate(): oper_real = jnp.take(tab_real, operator_index, axis=0)  37.9 us
    gather x3, local copies, waits for them, and re-layouts, translate(): pick_imag = jnp.take(pat_imag, source_index, axis=0)  37.8 us
    all_gather x1, blocking collectives, in_one_piece(): lax.all_gather(both, axis, axis=dim, tiled=True)  36.8 us
    all_to_all x1, starting transfers between devices, copy_for_each(): return lax.all_to_all(copies, axis, split_axis=0, concat_axis=0, tiled=True)  17.2 us
    all_to_all x1, blocking collectives, on_device(): lax.all_to_all(incoming, WIDE, split_axis=0, concat_axis=2, tiled=True)  11.8 us
    reduce_sum x1, other arithmetic, translate(): jnp.sum(weight * (oper_real * pick_real - oper_imag * pick_imag), 1)  11.1 us
  transfers between devices with their start and end apart: 3, of which 1 were waited for; matrix products, arithmetic and copies ran while one was open for 29% of the time, Pallas kernels for 0%

commit v1 on v0

v1 whole, which is shorter than its diff:
```python
import functools

import jax
import jax.numpy as jnp
from jax import lax
from jax.experimental import pallas as pl
from jax.experimental.pallas import tpu as pltpu
from jax.sharding import PartitionSpec as P

MESH = pl.DeviceIdType.MESH
BF16 = jnp.bfloat16
F32 = jnp.float32
LANES = 128
GROUP = 8
NO_OPERATOR = 511


def kernel(
    dims,
    counts_ref, coef_ref, rad_hbm, int_hbm, ang_ref, tab_ref, src_ref, opr_ref,
    out_ref,
    rad, itp, cosv, sinv, work, outg, list_send, list_got, x_send, x_got, x_all,
    tab, onehot_x, onehot_t, acc, r_send, r_got, inc, recv_acc,
    mem_sem, list_ss, list_rs, x_ss, x_rs, n_ss, n_rs, r_ss, r_rs,
):
    n_wide, n_narrow, chunk = dims
    me_w = lax.axis_index("wide")
    me_n = lax.axis_index("narrow")
    q0, q1 = int_hbm.shape
    parts = q1 // chunk
    dirs = q1 // n_wide
    n_list = src_ref.shape[1]
    n_rows = 2 * n_wide

    rad_copy = pltpu.make_async_copy(rad_hbm, rad, mem_sem.at[parts])
    rad_copy.start()

    def int_copy(i):
        cols = pl.ds(pl.multiple_of(i * chunk, chunk), chunk)
        return pltpu.make_async_copy(int_hbm.at[:, cols], itp.at[:, cols], mem_sem.at[i])

    lax.fori_loop(0, parts, lambda i, c: (int_copy(i).start(), c)[1], 0)

    barrier = pltpu.get_barrier_semaphore()

    def wide_peer(k):
        return lax.rem(me_w + k, n_wide)

    def narrow_peer(k):
        return lax.rem(me_n + k, n_narrow)

    def greet_wide(k, c):
        pl.semaphore_signal(barrier, 1, device_id=(wide_peer(k), me_n), device_id_type=MESH)
        return c

    def greet_narrow(k, c):
        pl.semaphore_signal(barrier, 1, device_id=(me_w, narrow_peer(k)), device_id_type=MESH)
        return c

    lax.fori_loop(1, n_wide, greet_wide, 0)
    lax.fori_loop(1, n_narrow, greet_narrow, 0)

    src = src_ref[...]
    opr = opr_ref[...]
    half = lax.shift_right_logical(src, 1)
    row = (half % n_narrow) * n_rows + (half // n_narrow) * 2 + (src & 1)
    lane = lax.broadcasted_iota(jnp.int32, src.shape, 1)
    which = lax.broadcasted_iota(jnp.int32, src.shape, 0)
    limit = jnp.where(which == 0, counts_ref[0], counts_ref[1])
    packed = row * 512 + jnp.where(lane < limit, opr, NO_OPERATOR)
    list_send[...] = jnp.full(list_send.shape, NO_OPERATOR, jnp.int32)
    list_send[:, pl.ds(0, n_list)] = packed

    work_t = jnp.zeros((2 * LANES, tab.shape[0]), F32)
    n_ops = tab_ref.shape[2]
    for c in range(2):
        t = tab_ref[c]
        t = jnp.concatenate([t, jnp.zeros((LANES - dirs, n_ops), F32)], 0)
        t = jnp.concatenate([t, jnp.zeros((LANES, tab.shape[0] - n_ops), F32)], 1)
        tab[:, pl.ds(c * LANES, LANES)] = t.T.astype(BF16)

    rad_copy.wait()
    half_rows = coef_ref.shape[0] // 2
    work[...] = lax.dot_general(
        rad[...], coef_ref[...], (((1,), (1,)), ((), ())), preferred_element_type=F32
    )
    by_real = work[pl.ds(0, q0, stride=2), :]
    by_imag = work[pl.ds(1, q0, stride=2), :]
    leaf_t = jnp.concatenate(
        [
            by_real[:, :half_rows] - by_imag[:, half_rows:],
            by_imag[:, :half_rows] + by_real[:, half_rows:],
        ],
        1,
    )
    leaf = leaf_t.T.astype(BF16)

    def up_chunk(i, c):
        cols = pl.ds(pl.multiple_of(i * chunk, chunk), chunk)
        ang = ang_ref[:, cols]
        co = jnp.cos(ang)
        si = jnp.sin(ang)
        cosv[:, cols] = co
        sinv[:, cols] = si
        int_copy(i).wait()
        up = jnp.dot(leaf, itp[:, cols], preferred_element_type=F32)
        for p in range(2):
            ur = up[8 * p : 8 * p + 8]
            ui = up[16 + 8 * p : 24 + 8 * p]
            outg[pl.ds(p, 1), cols] = jnp.sum(co * ur - si * ui, 0, keepdims=True)
            outg[pl.ds(2 + p, 1), cols] = jnp.sum(co * ui + si * ur, 0, keepdims=True)
        return c

    lax.fori_loop(0, parts, up_chunk, 0)

    pl.semaphore_wait(barrier, n_wide - 1 + n_narrow - 1)

    def list_out(k):
        return pltpu.make_async_remote_copy(
            src_ref=list_send, dst_ref=list_got.at[me_w], send_sem=list_ss.at[k],
            recv_sem=list_rs.at[me_w], device_id=(wide_peer(k), me_n), device_id_type=MESH)

    def list_in(k):
        w = wide_peer(k)
        return pltpu.make_async_remote_copy(
            src_ref=list_send, dst_ref=list_got.at[w], send_sem=list_ss.at[k],
            recv_sem=list_rs.at[w], device_id=(w, me_n), device_id_type=MESH)

    for w in range(n_wide):
        tile, off = divmod(w * dirs, LANES)
        piece = outg[:, pl.ds(tile * LANES, LANES)]
        if off:
            piece = pltpu.roll(piece, LANES - off, 1)
            if off + dirs > LANES:
                more = pltpu.roll(outg[:, pl.ds((tile + 1) * LANES, LANES)], LANES - off, 1)
                at = lax.broadcasted_iota(jnp.int32, piece.shape, 1)
                piece = jnp.where(at < LANES - off, piece, more)
        x_send[w, :, pl.ds(0, LANES)] = piece[0:2]
        x_send[w, :, pl.ds(LANES, LANES)] = piece[2:4]

    def x_out(k):
        w = wide_peer(k)
        return pltpu.make_async_remote_copy(
            src_ref=x_send.at[w], dst_ref=x_got.at[me_w], send_sem=x_ss.at[k],
            recv_sem=x_rs.at[me_w], device_id=(w, me_n), device_id_type=MESH)

    def x_in(k):
        w = wide_peer(k)
        return pltpu.make_async_remote_copy(
            src_ref=x_send.at[w], dst_ref=x_got.at[w], send_sem=x_ss.at[k],
            recv_sem=x_rs.at[w], device_id=(w, me_n), device_id_type=MESH)

    def start(make):
        return lambda k, c: (make(k).start(), c)[1]

    def got(make):
        return lambda k, c: (make(k).wait_recv(), c)[1]

    def sent(make):
        return lambda k, c: (make(k).wait_send(), c)[1]

    lax.fori_loop(1, n_wide, start(x_out), 0)
    lax.fori_loop(1, n_wide, start(list_out), 0)
    x_got[me_w] = x_send[me_w]
    list_got[me_w] = list_send[...]
    lax.fori_loop(1, n_wide, got(x_in), 0)
    x_all[me_n] = x_got[...].reshape(n_rows, 2 * LANES)

    def n_out(k):
        return pltpu.make_async_remote_copy(
            src_ref=x_all.at[me_n], dst_ref=x_all.at[me_n], send_sem=n_ss.at[k],
            recv_sem=n_rs.at[me_n], device_id=(me_w, narrow_peer(k)), device_id_type=MESH)

    def n_in(k):
        n = narrow_peer(k)
        return pltpu.make_async_remote_copy(
            src_ref=x_all.at[me_n], dst_ref=x_all.at[n], send_sem=n_ss.at[k],
            recv_sem=n_rs.at[n], device_id=(me_w, n), device_id_type=MESH)

    lax.fori_loop(1, n_narrow, start(n_out), 0)
    lax.fori_loop(1, n_wide, got(list_in), 0)
    lists = list_got[...]
    lists = [lists[:, :, t * LANES : (t + 1) * LANES].reshape(n_rows, LANES) for t in range(2)]
    lax.fori_loop(1, n_narrow, got(n_in), 0)
    rows_all = n_narrow * n_rows
    pat = x_all[...].astype(BF16).reshape(rows_all, 2 * LANES)

    acc[...] = jnp.zeros(acc.shape, F32)
    at_x = lax.broadcasted_iota(jnp.int32, (n_rows, rows_all), 1)
    at_t = lax.broadcasted_iota(jnp.int32, (n_rows, tab.shape[0]), 1)
    for t in range(2):
        held = lists[t]
        steps = -(-min(n_list - t * LANES, LANES) // GROUP)

        def step(i, c, held=held):
            here = pltpu.roll(held, lax.rem(LANES - i * GROUP, LANES), 1)
            for u in range(GROUP):
                entry = here[:, u : u + 1]
                source = lax.shift_right_logical(entry, 9)
                oper = entry & 511
                rows = pl.ds(u * n_rows, n_rows)
                onehot_x[rows, :] = jnp.where(source == at_x, 1.0, 0.0).astype(BF16)
                onehot_t[rows, :] = jnp.where(oper == at_t, 1.0, 0.0).astype(BF16)
            px = jnp.dot(onehot_x[...], pat, preferred_element_type=F32)
            pt = jnp.dot(onehot_t[...], tab[...], preferred_element_type=F32)
            xr, xi = px[:, :LANES], px[:, LANES:]
            tr, ti = pt[:, :LANES], pt[:, LANES:]
            real = (tr * xr - ti * xi).reshape(GROUP, n_rows, LANES).sum(0)
            imag = (tr * xi + ti * xr).reshape(GROUP, n_rows, LANES).sum(0)
            acc[:, pl.ds(0, LANES)] += real
            acc[:, pl.ds(LANES, LANES)] += imag
            return c

        lax.fori_loop(0, steps, step, 0)

    r_send[...] = acc[...].reshape(n_wide, 2, 2 * LANES)

    def r_out(k):
        w = wide_peer(k)
        return pltpu.make_async_remote_copy(
            src_ref=r_send.at[w], dst_ref=r_got.at[me_w], send_sem=r_ss.at[k],
            recv_sem=r_rs.at[me_w], device_id=(w, me_n), device_id_type=MESH)

    def r_in(k):
        w = wide_peer(k)
        return pltpu.make_async_remote_copy(
            src_ref=r_send.at[w], dst_ref=r_got.at[w], send_sem=r_ss.at[k],
            recv_sem=r_rs.at[w], device_id=(w, me_n), device_id_type=MESH)

    lax.fori_loop(1, n_wide, start(r_out), 0)
    r_got[me_w] = r_send[me_w]
    recv_acc[...] = jnp.zeros(recv_acc.shape, F32)
    lax.fori_loop(1, n_wide, got(r_in), 0)

    tiles = [None] * (q1 // LANES)
    at = lax.broadcasted_iota(jnp.int32, (4, LANES), 1)
    for w in range(n_wide):
        tile, off = divmod(w * dirs, LANES)
        piece = jnp.concatenate(
            [r_got[w, :, pl.ds(0, LANES)], r_got[w, :, pl.ds(LANES, LANES)]], 0
        )
        if off:
            piece = pltpu.roll(piece, off, 1)
        if tiles[tile] is None:
            tiles[tile] = piece
        else:
            tiles[tile] = jnp.where(at < off, tiles[tile], piece)
        if off + dirs > LANES:
            tiles[tile + 1] = piece
    for i, tile in enumerate(tiles):
        inc[:, pl.ds(i * LANES, LANES)] = tile

    def down_chunk(i, c):
        cols = pl.ds(pl.multiple_of(i * chunk, chunk), chunk)
        co = cosv[:, cols]
        si = sinv[:, cols]
        real, imag = [], []
        for p in range(2):
            ir = inc[pl.ds(p, 1), cols]
            ii = inc[pl.ds(2 + p, 1), cols]
            real.append(co * ir + si * ii)
            imag.append(co * ii - si * ir)
        down = jnp.concatenate(real + imag, 0).astype(BF16)
        recv_acc[...] += lax.dot_general(
            itp[:, cols], down, (((1,), (1,)), ((), ())), preferred_element_type=F32
        )
        return c

    lax.fori_loop(0, parts, down_chunk, 0)

    got_t = recv_acc[...]
    work[pl.ds(0, q0, stride=2), :] = got_t
    work[pl.ds(1, q0, stride=2), :] = jnp.concatenate(
        [got_t[:, half_rows:], -got_t[:, :half_rows]], 1
    )
    out_ref[...] = jnp.dot(
        work[...].T.astype(BF16), rad[...], preferred_element_type=F32
    )

    for make in (list_out, x_out, r_out):
        lax.fori_loop(1, n_wide, sent(make), 0)
    lax.fori_loop(1, n_narrow, sent(n_out), 0)


def solution(mesh):
    n_wide, n_narrow = mesh.shape["wide"], mesh.shape["narrow"]
    both = ("wide", "narrow")

    def on_device(coef, rad, interp, angles, table, sources, operators, counts):
        boxes, _, n_bases = coef.shape
        q0, q1 = interp.shape
        n_ops = table.shape[0]
        chunk = 256 if q1 % 256 == 0 else 128
        parts = q1 // chunk
        rows = 2 * n_wide
        coef_rows = jnp.transpose(coef, (1, 0, 2)).reshape(2 * boxes, n_bases)
        rad_rows = jnp.transpose(rad, (2, 0, 1)).reshape(2 * q0, n_bases)
        table_t = jnp.transpose(table, (1, 2, 0))
        n_tab = -(-n_ops // LANES) * LANES
        vmem = pl.BlockSpec(memory_space=pltpu.VMEM)
        anyw = pl.BlockSpec(memory_space=pl.ANY)
        smem = pl.BlockSpec(memory_space=pltpu.SMEM)
        dma = pltpu.SemaphoreType.DMA
        result = pl.pallas_call(
            functools.partial(kernel, (n_wide, n_narrow, chunk)),
            out_shape=jax.ShapeDtypeStruct((2 * boxes, n_bases), F32),
            in_specs=[smem, vmem, anyw, anyw, vmem, vmem, vmem, vmem],
            out_specs=vmem,
            scratch_shapes=[
                pltpu.VMEM((2 * q0, n_bases), BF16),
                pltpu.VMEM((q0, q1), BF16),
                pltpu.VMEM((8, q1), F32),
                pltpu.VMEM((8, q1), F32),
                pltpu.VMEM((2 * q0, 2 * boxes), F32),
                pltpu.VMEM((4, q1), F32),
                pltpu.VMEM((2, 2 * LANES), jnp.int32),
                pltpu.VMEM((n_wide, 2, 2 * LANES), jnp.int32),
                pltpu.VMEM((n_wide, 2, 2 * LANES), F32),
                pltpu.VMEM((n_wide, 2, 2 * LANES), F32),
                pltpu.VMEM((n_narrow, rows, 2 * LANES), F32),
                pltpu.VMEM((n_tab, 2 * LANES), BF16),
                pltpu.VMEM((GROUP * rows, n_narrow * rows), BF16),
                pltpu.VMEM((GROUP * rows, n_tab), BF16),
                pltpu.VMEM((rows, 2 * LANES), F32),
                pltpu.VMEM((n_wide, 2, 2 * LANES), F32),
                pltpu.VMEM((n_wide, 2, 2 * LANES), F32),
                pltpu.VMEM((4, q1), F32),
                pltpu.VMEM((q0, 2 * boxes), F32),
                dma((parts + 1,)),
                dma((n_wide,)), dma((n_wide,)),
                dma((n_wide,)), dma((n_wide,)),
                dma((n_narrow,)), dma((n_narrow,)),
                dma((n_wide,)), dma((n_wide,)),
            ],
            compiler_params=pltpu.CompilerParams(
                collective_id=0, has_side_effects=True, vmem_limit_bytes=40 << 20
            ),
            name="fmm_step",
        )(counts, coef_rows, rad_rows, interp, angles, table_t, sources, operators)
        return jnp.transpose(result.reshape(2, boxes, n_bases), (1, 0, 2))

    return jax.shard_map(
        on_device,
        mesh=mesh,
        in_specs=(
            P(both, None, None), P(), P(), P(), P(None, None, "wide"),
            P(both, None), P(both, None), P(both),
        ),
        out_specs=P(both, None, None),
        check_vma=False,
    )
```

time: 268 us -> 61.9 us (0.23)
  local copies, waits for them, and re-layouts: 164 us -> 8.25 us
  Pallas kernels: 0 us -> 53.3 us
  blocking collectives: 48.6 us -> 0 us
  starting transfers between devices: 26.2 us -> 0 us
  other arithmetic: 12.6 us -> 0 us
  matrix products: 7.72 us -> 0 us
  waiting for transfers between devices: 6.51 us -> 0 us
    gather x12 -> x0, local copies, waits for them, and re-layouts: 152 us -> none  [the longest x3 38 us: translate(): oper_imag = jnp.take(tab_imag, operator_index, axis=0)]
    pallas_call x0 -> x1, Pallas kernels: none -> 53.3 us  [on_device(): pl.pallas_call(functools.partial(kernel, (n_wide, n_narrow, chunk)), out_...]
    all_gather x1 -> x0, blocking collectives: 36.8 us -> none  [in_one_piece(): lax.all_gather(both, axis, axis=dim, tiled=True)]
    all_to_all x3 -> x0, starting transfers between devices: 26.2 us -> none  [the longest x1 17.2 us: copy_for_each(): return lax.all_to_all(copies, axis, split_axis=0, concat_axis=0, tiled=True)]
    all_to_all x1 -> x0, blocking collectives: 11.8 us -> none  [on_device(): lax.all_to_all(incoming, WIDE, split_axis=0, concat_axis=2, tiled=True)]
    reduce_sum x2 -> x0, other arithmetic: 11.3 us -> none  [the longest x1 11.1 us: translate(): jnp.sum(weight * (oper_real * pick_real - oper_imag * pick_imag), 1)]
    dot_general x10 -> x0, matrix products: 7.72 us -> none  [the longest x1 4.46 us: on_device(): lax.dot_general(downward.reshape(box_dev * 2, parent_dirs), interpolation...]
    all_to_all x3 -> x0, waiting for transfers between devices: 6.51 us -> none  [the longest x2 6.51 us: turned_blocks(): lax.all_to_all(tiles, axes[k], split_axis=k, concat_axis=k, tiled=True)]
  transfers between devices with their start and end apart: 3 -> 0, of which waited for: 1 -> 0; matrix products, arithmetic and copies ran while one was open for 29% -> 0% of each run, Pallas kernels for 0% -> 0%
where the time goes in v1:
time: 61.9 us; the launch traced here: 61.6 us
  Pallas kernels  53.3 us (86%)
  local copies, waits for them, and re-layouts  8.25 us (13%)
    pallas_call x1, Pallas kernels, on_device(): pl.pallas_call(functools.partial(kernel, (n_wide, n_narrow, chunk)), out_...  53.3 us
    reshape x1, local copies, waits for them, and re-layouts, on_device(): rad_rows = jnp.transpose(rad, (2, 0, 1)).reshape(2 * q0, n_bases)  4.1 us
    unnamed x12, local copies, waits for them, and re-layouts  2.7 us

profile of v1, /device:TPU:1, one launch (start us, length us, event | category | flops | bytes accessed | tf_op | source)
XLA Modules:
  0.0 61.6 jit_solution(5307490959766149731)
XLA Ops:
  0.0 0.8 %copy.9 = bf16[2,16,512]{2,1,0:T(8,128)(2,1)S(1)} copy(bf16[2,16,512]{2,0,1:T(2,128)(2,1)} %bitcast.12) | data formatting | bytes 65536 | tf_op jit(solution)/shard_map/transpose | solution.py:296
  0.8 0.0 copy-start.1
  0.8 0.0 copy-start.2
  0.8 0.0 copy-start.3
  0.8 0.0 copy-start.4
  0.8 0.0 copy-start.5
  0.8 4.1 %reshape.10.rad_hbm = bf16[1764,512]{1,0:T(8,128)(2,1)S(1)} reshape(bf16[882,2,512]{2,1,0:T(2,128)(2,1)} %bitcast.11) | data formatting | bytes 3612672 | tf_op jit(solution)/shard_map/reshape | solution.py:297
  4.9 0.0 copy-done.1
  4.9 0.0 copy-done.2
  4.9 0.0 copy-done.3
  5.0 0.0 copy-done.4
  5.0 0.0 copy-done.5
  5.0 0.0 copy-start
  5.0 2.7 %copy-done = bf16[882,3328]{1,0:T(8,128)(2,1)S(1)} copy-done((bf16[882,3328]{1,0:T(8,128)(2,1)S(1)}, bf16[882,3328]{1,0:T(8,128)(2,1)}, u32[]{:S(2)}) %copy-start) | copy-done | bytes 5870616
  7.7 53.3 %fmm_step.1 = f32[32,512]{1,0:T(8,128)S(1)} custom-call(s32[2]{0:T(128)S(1)} %copy-done.5, bf16[32,512]{1,0:T(8,128)(2,1)S(1)} %bitcast.10, bf16[1764,512]{1,0:T(8,128)(2,1)S(1)} %reshape.10.rad_hbm, bf16[882,3328]{1,0:T(8,128)(2,1)S(1)} %copy-done, f32[8,3328]{1,0:T(8,128)S(1)} %copy-done.2, f32[2,104,316]{2,1,0:T(8,128)S(1)} %bitcast.8, ...), custom_call_target="tpu_custom_call" | custom-call | tf_op jit(solution)/shard_map/fmm_step/pallas_call | solution.py:304
  61.0 0.7 %copy.12 = f32[2,16,512]{2,0,1:T(2,128)} copy(f32[2,16,512]{2,1,0:T(8,128)S(1)} %bitcast.9) | data formatting | bytes 131072 | tf_op jit(solution)/shard_map/reshape | solution.py:340
Async XLA Ops:
  0.8 4.2 %copy-start.1 = (f32[316,2,104]{0,2,1:T(8,128)S(1)}, f32[316,2,104]{0,2,1:T(8,128)}, u32[]{:S(2)}) copy-start(f32[316,2,104]{0,2,1:T(8,128)} %param.12) | copy-start | bytes 788740
  0.8 4.2 %copy-start.2 = (f32[8,3328]{1,0:T(8,128)S(1)}, f32[8,3328]{1,0:T(8,128)}, u32[]{:S(2)}) copy-start(f32[8,3328]{1,0:T(8,128)} %ang_ref.1) | copy-start | bytes 319492
  0.8 4.2 %copy-start.3 = (s32[2,189]{1,0:T(2,128)S(1)}, s32[2,189]{1,0:T(2,128)}, u32[]{:S(2)}) copy-start(s32[2,189]{1,0:T(2,128)} %src_ref.1) | copy-start | bytes 4540
  0.8 4.2 %copy-start.4 = (s32[2,189]{1,0:T(2,128)S(1)}, s32[2,189]{1,0:T(2,128)}, u32[]{:S(2)}) copy-start(s32[2,189]{1,0:T(2,128)} %opr_ref.1) | copy-start | bytes 4540
  0.8 4.2 %copy-start.5 = (s32[2]{0:T(128)S(1)}, s32[2]{0:T(128)}, u32[]{:S(2)}) copy-start(s32[2]{0:T(128)} %counts_ref.1) | copy-start | bytes 28
  5.0 2.7 %copy-start = (bf16[882,3328]{1,0:T(8,128)(2,1)S(1)}, bf16[882,3328]{1,0:T(8,128)(2,1)}, u32[]{:S(2)}) copy-start(bf16[882,3328]{1,0:T(8,128)(2,1)} %int_hbm.1) | copy-start | bytes 17611780

commit v2 on v1

v2 whole, which is shorter than its diff:
```python
import functools

import jax
import jax.numpy as jnp
from jax import lax
from jax.experimental import pallas as pl
from jax.experimental.pallas import tpu as pltpu
from jax.sharding import PartitionSpec as P

MESH = pl.DeviceIdType.MESH
BF16 = jnp.bfloat16
F32 = jnp.float32
LANES = 128
GROUP = 32
HALVES = 2
NO_OPERATOR = 511


def offsets_along(n_x, n_z):
    def hops(o):
        return min(o[0], n_x - o[0]) + min(o[1], n_z - o[1])

    return sorted(((a, b) for a in range(n_x) for b in range(n_z)), key=lambda o: (-hops(o), o))


def kernel(
    dims,
    counts_ref, coef_ref, rad_hbm, int_hbm, ang_ref, tab_ref, src_ref, opr_ref,
    out_ref,
    raw, rad, itp, cosv, sinv, work, coefs, outg, list_send, list_got, lists, x_send, x_got, x_all,
    tab, picks, r_send, r_got, inc, recv_acc,
    mem_sem, list_ss, list_rs, x_ss, x_rs, n_ss, n_rs, r_ss, r_rs,
):
    n_wide, n_narrow, n_z, chunk = dims
    n_x = n_wide // n_z
    me_w = lax.axis_index("wide")
    me_n = lax.axis_index("narrow")
    me_x, me_z = me_w // n_z, me_w % n_z
    q0, q1 = int_hbm.shape
    parts = q1 // chunk
    dirs = q1 // n_wide
    n_list = src_ref.shape[1]
    n_rows = 2 * n_wide
    per_half = n_rows // HALVES
    per_tile = LANES // GROUP
    steps = -(-n_list // GROUP)
    boxes = coef_ref.shape[0]

    rad_copy = pltpu.make_async_copy(rad_hbm, raw, mem_sem.at[parts])
    rad_copy.start()

    def int_copy(i):
        cols = pl.ds(i * chunk, chunk)
        return pltpu.make_async_copy(int_hbm.at[:, cols], itp.at[:, cols], mem_sem.at[i])

    for i in range(parts):
        int_copy(i).start()

    barrier = pltpu.get_barrier_semaphore()
    offsets = offsets_along(n_x, n_z)
    place = {o: i for i, o in enumerate(offsets)}
    peers = []
    for dx, dz in offsets:
        w = lax.rem(me_x + dx, n_x) * n_z + lax.rem(me_z + dz, n_z)
        peers.append((w, place[(-dx) % n_x, (-dz) % n_z]))
    for w, _ in peers[:-1]:
        pl.semaphore_signal(barrier, 1, device_id=(w, me_n), device_id_type=MESH)
    me_y, me_c = me_n // 2, me_n % 2
    n_y = n_narrow // 2
    ahead = 1 - 2 * me_c
    n_up = lax.rem(me_y + ahead + n_y, n_y) * 2 + me_c
    n_dn = lax.rem(me_y - ahead + n_y, n_y) * 2 + me_c
    n_far = lax.rem(me_y + 2, n_y) * 2 + me_c
    n_par = me_y * 2 + 1 - me_c
    for n in (n_up, n_dn, n_par):
        pl.semaphore_signal(barrier, 1, device_id=(me_w, n), device_id_type=MESH)

    src = src_ref[...]
    opr = opr_ref[...]
    half = lax.shift_right_logical(src, 1)
    row = (half % n_narrow) * n_rows + (half // n_narrow) * 2 + (src & 1)
    lane = lax.broadcasted_iota(jnp.int32, src.shape, 1)
    which = lax.broadcasted_iota(jnp.int32, src.shape, 0)
    limit = jnp.where(which == 0, counts_ref[0], counts_ref[1])
    packed = row * 512 + jnp.where(lane < limit, opr, NO_OPERATOR)
    list_send[...] = jnp.full(list_send.shape, NO_OPERATOR, jnp.int32)
    list_send[:, pl.ds(0, n_list)] = packed

    n_ops = tab_ref.shape[2]
    for c in range(2):
        t = tab_ref[c]
        t = jnp.concatenate([t, jnp.zeros((LANES - dirs, n_ops), F32)], 0)
        t = jnp.concatenate([t, jnp.zeros((LANES, tab.shape[0] - n_ops), F32)], 1)
        tab[:, pl.ds(c * LANES, LANES)] = t.T.astype(BF16)

    tiled = coef_ref[...].astype(F32).reshape(2 * boxes, -1)
    bases = range(coefs.shape[0])
    for t in bases:
        coefs[t] = tiled[:, t * LANES : (t + 1) * LANES]
    coef = jnp.concatenate(
        [
            jnp.concatenate([coefs[t, pl.ds(c, boxes, stride=2), :] for t in bases], 1)
            for c in range(2)
        ],
        0,
    ).astype(BF16)

    rad_copy.wait()
    rad[...] = raw[...].reshape(rad.shape)
    work[...] = lax.dot_general(
        rad[...], coef, (((1,), (1,)), ((), ())), preferred_element_type=F32
    )
    by_real = work[pl.ds(0, q0, stride=2), :]
    by_imag = work[pl.ds(1, q0, stride=2), :]
    leaf_t = jnp.concatenate(
        [by_real[:, :boxes] - by_imag[:, boxes:], by_imag[:, :boxes] + by_real[:, boxes:]], 1
    )
    leaf = leaf_t.T.astype(BF16)

    def up_chunk(i):
        cols = pl.ds(i * chunk, chunk)
        ang = ang_ref[:, cols]
        co = jnp.cos(ang)
        si = jnp.sin(ang)
        cosv[:, cols] = co
        sinv[:, cols] = si
        int_copy(i).wait()
        up = jnp.dot(leaf, itp[:, cols], preferred_element_type=F32)
        for p in range(2):
            ur = up[8 * p : 8 * p + 8]
            ui = up[boxes + 8 * p : boxes + 8 * p + 8]
            outg[pl.ds(p, 1), cols] = jnp.sum(co * ur - si * ui, 0, keepdims=True)
            outg[pl.ds(2 + p, 1), cols] = jnp.sum(co * ui + si * ur, 0, keepdims=True)

    early = parts * 3 // 4
    for i in range(early):
        up_chunk(i)

    pl.semaphore_wait(barrier, n_wide - 1 + 3)

    def list_copy(w, there):
        return pltpu.make_async_remote_copy(
            src_ref=list_send, dst_ref=list_got.at[there], send_sem=list_ss, recv_sem=list_rs,
            device_id=(w, me_n), device_id_type=MESH)

    for w, there in peers[:-1]:
        list_copy(w, there).start()
    list_got[n_wide - 1] = list_send[...]

    for i in range(early, parts):
        up_chunk(i)

    for w in range(n_wide):
        tile, off = divmod(w * dirs, LANES)
        piece = outg[:, pl.ds(tile * LANES, LANES)]
        if off:
            piece = pltpu.roll(piece, LANES - off, 1)
            if off + dirs > LANES:
                more = pltpu.roll(outg[:, pl.ds((tile + 1) * LANES, LANES)], LANES - off, 1)
                at = lax.broadcasted_iota(jnp.int32, piece.shape, 1)
                piece = jnp.where(at < LANES - off, piece, more)
        x_send[w, :, pl.ds(0, LANES)] = piece[0:2]
        x_send[w, :, pl.ds(LANES, LANES)] = piece[2:4]

    def slice_copy(src_all, dst_all, at, w, send_sem, recv_sem):
        return pltpu.make_async_remote_copy(
            src_ref=src_all.at[at], dst_ref=dst_all.at[me_w], send_sem=send_sem,
            recv_sem=recv_sem, device_id=(w, me_n), device_id_type=MESH)

    def all_of(src_all, dst_all, send_sem, recv_sem):
        most = pl.ds(0, n_wide - 1)
        return pltpu.make_async_remote_copy(
            src_ref=src_all.at[most], dst_ref=dst_all.at[most], send_sem=send_sem,
            recv_sem=recv_sem, device_id=(peers[0][0], me_n), device_id_type=MESH)

    for w, _ in peers[:-1]:
        slice_copy(x_send, x_got, w, w, x_ss, x_rs).start()
    x_got[me_w] = x_send[me_w]

    all_of(list_got, list_got, list_ss, list_rs).wait_recv()
    for h in range(HALVES):
        mine = slice(h * n_wide // HALVES, (h + 1) * n_wide // HALVES)
        for t in range(2):
            lists[h, t] = list_got[mine, :, t * LANES : (t + 1) * LANES].reshape(per_half, LANES)

    def entries(g):
        s = g % steps
        held = lists[g // steps, s // per_tile]
        here = pltpu.roll(held, lax.rem(LANES - s % per_tile * GROUP, LANES), 1)
        columns = [here[:, u : u + 1] for u in range(GROUP)]
        return jnp.concatenate([jnp.broadcast_to(c, (per_half, LANES)) for c in columns], 0)

    lane_at = lax.broadcasted_iota(jnp.int32, (GROUP * per_half, LANES), 1)

    def one_hot(index, n):
        tiles = [jnp.where(index == lane_at + t, 1.0, 0.0).astype(BF16) for t in range(0, n, LANES)]
        return jnp.concatenate(tiles, 1)

    def pick_operators(g, c):
        onehot = one_hot(entries(g) & 511, tab.shape[0])
        picks[g] = jnp.dot(onehot, tab[...], preferred_element_type=F32).astype(BF16)
        return c

    total = HALVES * steps
    cuts = [0, total // 6, total * 7 // 12, total]
    lax.fori_loop(cuts[0], cuts[1], pick_operators, 0)

    all_of(x_got, x_got, x_ss, x_rs).wait_recv()
    x_all[me_n] = x_got[...].reshape(n_rows, 2 * LANES)

    def block_copy(k, block, to):
        return pltpu.make_async_remote_copy(
            src_ref=x_all.at[block], dst_ref=x_all.at[block], send_sem=n_ss.at[k],
            recv_sem=n_rs.at[block], device_id=(me_w, to), device_id_type=MESH)

    moves = [
        block_copy(0, me_n, n_up), block_copy(1, me_n, n_dn), block_copy(2, me_n, n_par),
        block_copy(3, n_dn, n_up), block_copy(4, n_dn, n_par), block_copy(5, n_up, n_par),
        block_copy(6, n_far, n_par),
    ]
    for m in moves[:3]:
        m.start()
    lax.fori_loop(cuts[1], cuts[2], pick_operators, 0)
    block_copy(0, n_dn, n_up).wait_recv()
    moves[3].start()
    moves[4].start()
    block_copy(0, n_up, n_up).wait_recv()
    moves[5].start()
    lax.fori_loop(cuts[2], cuts[3], pick_operators, 0)
    block_copy(0, n_far, n_up).wait_recv()
    moves[6].start()
    for y in range(n_y):
        block_copy(0, y * 2 + 1 - me_c, n_par).wait_recv()
    rows_all = n_narrow * n_rows
    pat = x_all[...].astype(BF16).reshape(rows_all, 2 * LANES)

    def translate(g, c):
        onehot = one_hot(lax.shift_right_logical(entries(g), 9), rows_all)
        px = jnp.dot(onehot, pat, preferred_element_type=F32)
        pt = picks[g].astype(F32)
        xr, xi = px[:, :LANES], px[:, LANES:]
        tr, ti = pt[:, :LANES], pt[:, LANES:]
        real = (tr * xr - ti * xi).reshape(GROUP, per_half, LANES).sum(0)
        imag = (tr * xi + ti * xr).reshape(GROUP, per_half, LANES).sum(0)
        return c[0] + real, c[1] + imag

    for h in range(HALVES):
        zero = jnp.zeros((per_half, LANES), F32)
        real, imag = lax.fori_loop(h * steps, (h + 1) * steps, translate, (zero, zero))
        mine = slice(h * n_wide // HALVES, (h + 1) * n_wide // HALVES)
        r_send[mine, :, pl.ds(0, LANES)] = real.reshape(-1, 2, LANES)
        r_send[mine, :, pl.ds(LANES, LANES)] = imag.reshape(-1, 2, LANES)
        for i in range(mine.start, min(mine.stop, n_wide - 1)):
            slice_copy(r_send, r_got, i, peers[i][0], r_ss, r_rs).start()
    r_got[me_w] = r_send[n_wide - 1]
    recv_acc[...] = jnp.zeros(recv_acc.shape, F32)
    all_of(r_got, r_got, r_ss, r_rs).wait_recv()

    tiles = [None] * (q1 // LANES)
    at = lax.broadcasted_iota(jnp.int32, (4, LANES), 1)
    for w in range(n_wide):
        tile, off = divmod(w * dirs, LANES)
        piece = jnp.concatenate(
            [r_got[w, :, pl.ds(0, LANES)], r_got[w, :, pl.ds(LANES, LANES)]], 0
        )
        if off:
            piece = pltpu.roll(piece, off, 1)
        if tiles[tile] is None:
            tiles[tile] = piece
        else:
            tiles[tile] = jnp.where(at < off, tiles[tile], piece)
        if off + dirs > LANES:
            tiles[tile + 1] = piece
    for i, tile in enumerate(tiles):
        inc[:, pl.ds(i * LANES, LANES)] = tile

    def down_chunk(i, c):
        cols = pl.ds(pl.multiple_of(i * chunk, chunk), chunk)
        co = cosv[:, cols]
        si = sinv[:, cols]
        real, imag = [], []
        for p in range(2):
            ir = inc[pl.ds(p, 1), cols]
            ii = inc[pl.ds(2 + p, 1), cols]
            real.append(co * ir + si * ii)
            imag.append(co * ii - si * ir)
        down = jnp.concatenate(real + imag, 0).astype(BF16)
        recv_acc[...] += lax.dot_general(
            itp[:, cols], down, (((1,), (1,)), ((), ())), preferred_element_type=F32
        )
        return c

    lax.fori_loop(0, parts, down_chunk, 0)

    got_t = recv_acc[...]
    work[pl.ds(0, q0, stride=2), :] = got_t
    work[pl.ds(1, q0, stride=2), :] = jnp.concatenate([got_t[:, boxes:], -got_t[:, :boxes]], 1)
    result = jnp.dot(work[...].T.astype(BF16), rad[...], preferred_element_type=F32)
    for t in bases:
        cols = slice(t * LANES, (t + 1) * LANES)
        coefs[t, pl.ds(0, boxes, stride=2), :] = result[:boxes, cols]
        coefs[t, pl.ds(1, boxes, stride=2), :] = result[boxes:, cols]
        out_ref[:, :, pl.ds(t * LANES, LANES)] = coefs[t].reshape(boxes, 2, LANES)

    all_of(list_got, list_got, list_ss, list_rs).wait_send()
    all_of(x_send, x_got, x_ss, x_rs).wait_send()
    all_of(r_send, r_got, r_ss, r_rs).wait_send()
    for m in moves:
        m.wait_send()


def solution(mesh):
    n_wide, n_narrow = mesh.shape["wide"], mesh.shape["narrow"]
    n_z = 8
    both = ("wide", "narrow")

    def on_device(coef, rad, interp, angles, table, sources, operators, counts):
        boxes, _, n_bases = coef.shape
        q0, q1 = interp.shape
        n_ops = table.shape[0]
        n_list = sources.shape[1]
        chunk = 256
        parts = q1 // chunk
        rows = 2 * n_wide
        rad_raw = jnp.transpose(rad, (2, 0, 1))
        table_t = jnp.transpose(table, (1, 2, 0))
        n_tab = -(-n_ops // LANES) * LANES
        steps = -(-n_list // GROUP)
        vmem = pl.BlockSpec(memory_space=pltpu.VMEM)
        anyw = pl.BlockSpec(memory_space=pl.ANY)
        smem = pl.BlockSpec(memory_space=pltpu.SMEM)
        dma = pltpu.SemaphoreType.DMA
        slots = (n_wide, 2, 2 * LANES)
        return pl.pallas_call(
            functools.partial(kernel, (n_wide, n_narrow, n_z, chunk)),
            out_shape=jax.ShapeDtypeStruct((boxes, 2, n_bases), F32),
            in_specs=[smem, vmem, anyw, anyw, vmem, vmem, vmem, vmem],
            out_specs=vmem,
            scratch_shapes=[
                pltpu.VMEM((q0, 2, n_bases), BF16),
                pltpu.VMEM((2 * q0, n_bases), BF16),
                pltpu.VMEM((q0, q1), BF16),
                pltpu.VMEM((8, q1), F32),
                pltpu.VMEM((8, q1), F32),
                pltpu.VMEM((2 * q0, 2 * boxes), F32),
                pltpu.VMEM((n_bases // LANES, 2 * boxes, LANES), F32),
                pltpu.VMEM((4, q1), F32),
                pltpu.VMEM((2, 2 * LANES), jnp.int32),
                pltpu.VMEM(slots, jnp.int32),
                pltpu.VMEM((HALVES, 2, rows // HALVES, LANES), jnp.int32),
                pltpu.VMEM(slots, F32),
                pltpu.VMEM(slots, F32),
                pltpu.VMEM((n_narrow, rows, 2 * LANES), F32),
                pltpu.VMEM((n_tab, 2 * LANES), BF16),
                pltpu.VMEM((HALVES * steps, GROUP * rows // HALVES, 2 * LANES), BF16),
                pltpu.VMEM(slots, F32),
                pltpu.VMEM(slots, F32),
                pltpu.VMEM((4, q1), F32),
                pltpu.VMEM((q0, 2 * boxes), F32),
                dma((parts + 1,)),
                dma, dma, dma, dma, dma((7,)), dma((n_narrow,)), dma, dma,
            ],
            compiler_params=pltpu.CompilerParams(
                collective_id=0, has_side_effects=True, vmem_limit_bytes=60 * 1024 * 1024
            ),
            name="fmm_step",
        )(counts, coef, rad_raw, interp, angles, table_t, sources, operators)

    return jax.shard_map(
        on_device,
        mesh=mesh,
        in_specs=(
            P(both, None, None), P(), P(), P(), P(None, None, "wide"),
            P(both, None), P(both, None), P(both),
        ),
        out_specs=P(both, None, None),
        check_vma=False,
    )
```

time: 61.9 us -> 46.2 us (0.75)
  Pallas kernels: 53.3 us -> 44.6 us
  local copies, waits for them, and re-layouts: 8.25 us -> 1.47 us
    pallas_call x1, Pallas kernels: 53.3 us -> 44.6 us  [on_device(): pl.pallas_call(functools.partial(kernel, (n_wide, n_narrow, n_z, chunk)),...]
    reshape x2 -> x0, local copies, waits for them, and re-layouts: 4.78 us -> none  [the longest x1 4.1 us: on_device(): rad_rows = jnp.transpose(rad, (2, 0, 1)).reshape(2 * q0, n_bases)]
    unnamed x12 -> x1, local copies, waits for them, and re-layouts: 2.7 us -> 1.47 us
    transpose x1 -> x0, local copies, waits for them, and re-layouts: 0.76 us -> none  [on_device(): coef_rows = jnp.transpose(coef, (1, 0, 2)).reshape(2 * boxes, n_bases)]
where the time goes in v2:
time: 46.2 us; the launch traced here: 46.1 us
  Pallas kernels  44.6 us (97%)
  local copies, waits for them, and re-layouts  1.47 us (3%)
    pallas_call x1, Pallas kernels, on_device(): pl.pallas_call(functools.partial(kernel, (n_wide, n_narrow, n_z, chunk)),...  44.6 us
    unnamed x1, local copies, waits for them, and re-layouts  1.47 us

profile of v2, /device:TPU:1, one launch (start us, length us, event | category | flops | bytes accessed | tf_op | source)
XLA Modules:
  0.0 46.1 jit_solution(14248643511499090327)
XLA Ops:
  0.0 44.6 %fmm_step.1 = f32[16,2,512]{2,1,0:T(2,128)} custom-call(s32[2]{0:T(128)} %counts_ref.1, bf16[16,2,512]{2,1,0:T(2,128)(2,1)} %coef_ref.1, bf16[882,2,512]{2,1,0:T(2,128)(2,1)} %bitcast.2, bf16[882,3328]{1,0:T(8,128)(2,1)} %int_hbm.1, f32[8,3328]{1,0:T(8,128)} %ang_ref.1, f32[2,104,316]{2,1,0:T(8,128)} %bitcast.3, s32[2,189]{1,0:T(2,128)} %src_ref.1, ...), custom_call_target="tpu_custom_call" | custom-call | tf_op jit(solution)/shard_map/fmm_step/pallas_call | solution.py:334
  44.6 1.5 %copy.10 = f32[16,2,512]{2,1,0:T(2,128)} copy(f32[16,2,512]{2,1,0:T(2,128)} %fmm_step.1) | data formatting | bytes 131072

commit v3 on v2

v3 whole, which is shorter than its diff:
```python
import functools

import jax
import jax.numpy as jnp
from jax import lax
from jax.experimental import pallas as pl
from jax.experimental.pallas import tpu as pltpu
from jax.sharding import PartitionSpec as P

MESH = pl.DeviceIdType.MESH
BF16 = jnp.bfloat16
F32 = jnp.float32
LANES = 128
GROUP = 96
STEPS = 2
SHARES = 4
CHUNKS = 2
NO_OPERATOR = 511


def offsets_along(n_x, n_z):
    def hops(o):
        return min(o[0], n_x - o[0]) + min(o[1], n_z - o[1])

    return sorted(((a, b) for a in range(n_x) for b in range(n_z)), key=lambda o: (-hops(o), o))


def kernel(
    dims,
    counts_hbm, coef_hbm, rad_hbm, int_hbm, ang_hbm, tab_hbm, src_hbm, opr_hbm,
    out_ref,
    counts_ref, coef_ref, ang_ref, tab_ref, src_ref, opr_ref,
    raw, rad, itp, cosv, sinv, work, coefs, outg, list_send, list_got, lists, x_send, x_got, x_all,
    tab, picks, down, r_send, r_got, inc, recv_acc,
    mem_sem, list_ss, list_rs, x_ss, x_rs, n_ss, n_rs, r_ss, r_rs,
):
    n_wide, n_narrow, n_z, chunk = dims
    n_x = n_wide // n_z
    me_w = lax.axis_index("wide")
    me_n = lax.axis_index("narrow")
    me_x, me_z = me_w // n_z, me_w % n_z
    q0, q1 = int_hbm.shape
    parts = q1 // chunk
    dirs = q1 // n_wide
    n_list = src_ref.shape[1]
    n_rows = 2 * n_wide
    per_share = n_rows // SHARES
    per_chunk = n_wide // CHUNKS
    boxes = coef_ref.shape[0]

    small = [
        pltpu.make_async_copy(a, b, mem_sem.at[parts + 1 + i])
        for i, (a, b) in enumerate([
            (ang_hbm, ang_ref), (coef_hbm, coef_ref), (src_hbm, src_ref), (opr_hbm, opr_ref),
            (counts_hbm, counts_ref), (tab_hbm, tab_ref),
        ])
    ]
    small[0].start()
    rad_copy = pltpu.make_async_copy(rad_hbm, raw, mem_sem.at[parts])
    rad_copy.start()
    for copy in small[1:]:
        copy.start()

    def int_copy(i):
        cols = pl.ds(i * chunk, chunk)
        return pltpu.make_async_copy(int_hbm.at[:, cols], itp.at[:, cols], mem_sem.at[i])

    for i in range(parts):
        int_copy(i).start()

    barrier = pltpu.get_barrier_semaphore()
    offsets = offsets_along(n_x, n_z)
    place = {o: i for i, o in enumerate(offsets)}
    peers = []
    for dx, dz in offsets:
        w = lax.rem(me_x + dx, n_x) * n_z + lax.rem(me_z + dz, n_z)
        peers.append((w, place[(-dx) % n_x, (-dz) % n_z]))
    for w, _ in peers[:-1]:
        pl.semaphore_signal(barrier, 1, device_id=(w, me_n), device_id_type=MESH)
    me_y, me_c = me_n // 2, me_n % 2
    n_y = n_narrow // 2
    ahead = 1 - 2 * me_c
    n_up = lax.rem(me_y + ahead + n_y, n_y) * 2 + me_c
    n_dn = lax.rem(me_y - ahead + n_y, n_y) * 2 + me_c
    n_far = lax.rem(me_y + 2, n_y) * 2 + me_c
    n_par = me_y * 2 + 1 - me_c
    n_cross = n_up + ahead
    for n in (n_up, n_dn, n_par, n_cross):
        pl.semaphore_signal(barrier, 1, device_id=(me_w, n), device_id_type=MESH)

    small[0].wait()
    for i in range(parts):
        cols = pl.ds(i * chunk, chunk)
        cosv[:, cols] = jnp.cos(ang_ref[:, cols])
        sinv[:, cols] = jnp.sin(ang_ref[:, cols])

    for copy in small[1:]:
        copy.wait()
    src = src_ref[...]
    opr = opr_ref[...]
    half = lax.shift_right_logical(src, 1)
    row = (half % n_narrow) * n_rows + (half // n_narrow) * 2 + (src & 1)
    lane = lax.broadcasted_iota(jnp.int32, src.shape, 1)
    which = lax.broadcasted_iota(jnp.int32, src.shape, 0)
    limit = jnp.where(which == 0, counts_ref[0], counts_ref[1])
    packed = row * 512 + jnp.where(lane < limit, opr, NO_OPERATOR)
    list_send[...] = jnp.full(list_send.shape, NO_OPERATOR, jnp.int32)
    list_send[:, pl.ds(0, GROUP)] = packed[:, :GROUP]
    list_send[:, pl.ds(LANES, n_list - GROUP)] = packed[:, GROUP:]

    n_ops = tab_ref.shape[2]
    for c in range(2):
        t = tab_ref[c]
        t = jnp.concatenate([t, jnp.zeros((LANES - dirs, n_ops), F32)], 0)
        t = jnp.concatenate([t, jnp.zeros((LANES, tab.shape[0] - n_ops), F32)], 1)
        tab[:, pl.ds(c * LANES, LANES)] = t.T.astype(BF16)

    tiled = coef_ref[...].astype(F32).reshape(2 * boxes, -1)
    bases = range(coefs.shape[0])
    for t in bases:
        coefs[t] = tiled[:, t * LANES : (t + 1) * LANES]
    coef = jnp.concatenate(
        [
            jnp.concatenate([coefs[t, pl.ds(c, boxes, stride=2), :] for t in bases], 1)
            for c in range(2)
        ],
        0,
    ).astype(BF16)

    rad_copy.wait()
    rad[...] = raw[...].reshape(rad.shape)
    work[...] = lax.dot_general(
        rad[...], coef, (((1,), (1,)), ((), ())), preferred_element_type=F32
    )
    by_real = work[pl.ds(0, q0, stride=2), :]
    by_imag = work[pl.ds(1, q0, stride=2), :]
    leaf_t = jnp.concatenate(
        [by_real[:, :boxes] - by_imag[:, boxes:], by_imag[:, :boxes] + by_real[:, boxes:]], 1
    )
    leaf = leaf_t.T.astype(BF16)

    def up_chunk(i):
        cols = pl.ds(i * chunk, chunk)
        co = cosv[:, cols]
        si = sinv[:, cols]
        int_copy(i).wait()
        up = jnp.dot(leaf, itp[:, cols], preferred_element_type=F32)
        for p in range(2):
            ur = up[8 * p : 8 * p + 8]
            ui = up[boxes + 8 * p : boxes + 8 * p + 8]
            outg[pl.ds(p, 1), cols] = jnp.sum(co * ur - si * ui, 0, keepdims=True)
            outg[pl.ds(2 + p, 1), cols] = jnp.sum(co * ui + si * ur, 0, keepdims=True)

    early = parts * 3 // 4
    for i in range(early):
        up_chunk(i)

    pl.semaphore_wait(barrier, n_wide - 1 + 4)

    def list_copy(w, there):
        return pltpu.make_async_remote_copy(
            src_ref=list_send, dst_ref=list_got.at[there], send_sem=list_ss, recv_sem=list_rs,
            device_id=(w, me_n), device_id_type=MESH)

    for w, there in peers[:-1]:
        list_copy(w, there).start()
    list_got[n_wide - 1] = list_send[...]

    for i in range(early, parts):
        up_chunk(i)

    for w in range(n_wide):
        tile, off = divmod(w * dirs, LANES)
        piece = outg[:, pl.ds(tile * LANES, LANES)]
        if off:
            piece = pltpu.roll(piece, LANES - off, 1)
            if off + dirs > LANES:
                more = pltpu.roll(outg[:, pl.ds((tile + 1) * LANES, LANES)], LANES - off, 1)
                at = lax.broadcasted_iota(jnp.int32, piece.shape, 1)
                piece = jnp.where(at < LANES - off, piece, more)
        x_send[w, :, pl.ds(0, LANES)] = piece[0:2]
        x_send[w, :, pl.ds(LANES, LANES)] = piece[2:4]

    def slice_copy(src_all, at, dst_all, there, w, send_sem, recv_sem):
        return pltpu.make_async_remote_copy(
            src_ref=src_all.at[at], dst_ref=dst_all.at[there], send_sem=send_sem,
            recv_sem=recv_sem, device_id=(w, me_n), device_id_type=MESH)

    def all_of(src_all, dst_all, send_sem, recv_sem, first=0, count=n_wide - 1):
        some = pl.ds(first, count)
        return pltpu.make_async_remote_copy(
            src_ref=src_all.at[some], dst_ref=dst_all.at[some], send_sem=send_sem,
            recv_sem=recv_sem, device_id=(peers[0][0], me_n), device_id_type=MESH)

    for w, there in peers[:-1]:
        slice_copy(x_send, w, x_got, there, w, x_ss, x_rs.at[there // per_chunk]).start()
    x_got[n_wide - 1] = x_send[me_w]

    lane_at = lax.broadcasted_iota(jnp.int32, (GROUP * per_share, LANES), 1)
    rows_all = n_narrow * n_rows
    spot = lax.broadcasted_iota(jnp.int32, (8, rows_all), 1)
    per_part = 2 * per_chunk
    place_of = (spot // (n_narrow * per_part)) * per_chunk + spot % per_part // 2
    holds = jnp.zeros((8, rows_all), jnp.int32)
    for i, (w, _) in enumerate(peers):
        holds = jnp.where(place_of == i, w, holds)
    holds = spot // per_part % n_narrow * n_rows + holds * 2 + spot % 2
    row_at = [
        jnp.broadcast_to(holds[0:1, t : t + LANES], (GROUP * per_share, LANES))
        for t in range(0, rows_all, LANES)
    ]

    all_of(list_got, list_got, list_ss, list_rs).wait_recv()
    for h in range(SHARES):
        mine = slice(h * n_wide // SHARES, (h + 1) * n_wide // SHARES)
        for t in range(STEPS):
            lists[h * STEPS + t] = list_got[mine, :, t * LANES : (t + 1) * LANES].reshape(
                per_share, LANES
            )

    def entries(g):
        here = lists[g]
        columns = [here[:, u : u + 1] for u in range(GROUP)]
        return jnp.concatenate([jnp.broadcast_to(c, (per_share, LANES)) for c in columns], 0)

    def one_hot(index, lanes):
        tiles = [jnp.where(index == at, 1.0, 0.0).astype(BF16) for at in lanes]
        return jnp.concatenate(tiles, 1)

    operators_at = [lane_at + t for t in range(0, tab.shape[0], LANES)]

    def pick_operators(g, c):
        onehot = one_hot(entries(g) & 511, operators_at)
        picks[g] = jnp.dot(onehot, tab[...], preferred_element_type=F32).astype(BF16)
        return c

    def pick(first, last):
        lax.fori_loop(first, last, pick_operators, 0)

    def block_copy(c, block, to):
        return pltpu.make_async_remote_copy(
            src_ref=x_all.at[c, block], dst_ref=x_all.at[c, block], send_sem=n_ss,
            recv_sem=n_rs.at[c * n_narrow + block], device_id=(me_w, to), device_id_type=MESH)

    def gather_slices(c):
        first = c * per_chunk
        count = per_chunk if c == 0 else per_chunk - 1
        all_of(x_got, x_got, x_ss, x_rs.at[c], first, count).wait_recv()
        x_all[c, me_n] = x_got[first : first + per_chunk].reshape(per_part, 2 * LANES)
        for to in (n_up, n_dn, n_par):
            block_copy(c, me_n, to).start()

    def pass_on(c):
        block_copy(c, n_dn, n_up).wait_recv()
        for to in (n_up, n_cross, n_par):
            block_copy(c, n_dn, to).start()
        block_copy(c, n_up, n_up).wait_recv()
        block_copy(c, n_up, n_par).start()

    pick(0, 1)
    gather_slices(1)
    pick(1, 2)
    gather_slices(0)
    pick(2, 3)
    pass_on(1)
    pick(3, 5)
    pass_on(0)
    pick(5, SHARES * STEPS)
    for c in range(CHUNKS):
        for n in (n_far, n_par, n_par + n_up - me_n, n_par + n_dn - me_n, n_par + n_far - me_n):
            block_copy(c, n, n_up).wait_recv()
    pat = x_all[...].astype(BF16).reshape(rows_all, 2 * LANES)

    def translate(g, c):
        onehot = one_hot(lax.shift_right_logical(entries(g), 9), row_at)
        px = jnp.dot(onehot, pat, preferred_element_type=F32)
        pt = picks[g].astype(F32)
        xr, xi = px[:, :LANES], px[:, LANES:]
        tr, ti = pt[:, :LANES], pt[:, LANES:]
        real = (tr * xr - ti * xi).reshape(GROUP, per_share, LANES).sum(0)
        imag = (tr * xi + ti * xr).reshape(GROUP, per_share, LANES).sum(0)
        return c[0] + real, c[1] + imag

    for h in range(SHARES):
        zero = jnp.zeros((per_share, LANES), F32)
        real, imag = lax.fori_loop(h * STEPS, (h + 1) * STEPS, translate, (zero, zero))
        mine = slice(h * n_wide // SHARES, (h + 1) * n_wide // SHARES)
        r_send[mine, :, pl.ds(0, LANES)] = real.reshape(-1, 2, LANES)
        r_send[mine, :, pl.ds(LANES, LANES)] = imag.reshape(-1, 2, LANES)
        for i in range(mine.start, min(mine.stop, n_wide - 1)):
            slice_copy(r_send, i, r_got, me_w, peers[i][0], r_ss, r_rs).start()
    r_got[me_w] = r_send[n_wide - 1]
    all_of(r_got, r_got, r_ss, r_rs).wait_recv()

    tiles = [None] * (q1 // LANES)
    at = lax.broadcasted_iota(jnp.int32, (4, LANES), 1)
    for w in range(n_wide):
        tile, off = divmod(w * dirs, LANES)
        piece = jnp.concatenate(
            [r_got[w, :, pl.ds(0, LANES)], r_got[w, :, pl.ds(LANES, LANES)]], 0
        )
        if off:
            piece = pltpu.roll(piece, off, 1)
        if tiles[tile] is None:
            tiles[tile] = piece
        else:
            tiles[tile] = jnp.where(at < off, tiles[tile], piece)
        if off + dirs > LANES:
            tiles[tile + 1] = piece
    for i, tile in enumerate(tiles):
        inc[:, pl.ds(i * LANES, LANES)] = tile

    for i in range(parts):
        cols = pl.ds(i * chunk, chunk)
        co = cosv[:, cols]
        si = sinv[:, cols]
        real, imag = [], []
        for p in range(2):
            ir = inc[pl.ds(p, 1), cols]
            ii = inc[pl.ds(2 + p, 1), cols]
            real.append(co * ir + si * ii)
            imag.append(co * ii - si * ir)
        down[:, cols] = jnp.concatenate(real + imag, 0).astype(BF16)
    recv_acc[...] = lax.dot_general(
        itp[...], down[...], (((1,), (1,)), ((), ())), preferred_element_type=F32
    )

    got_t = recv_acc[...]
    work[pl.ds(0, q0, stride=2), :] = got_t
    work[pl.ds(1, q0, stride=2), :] = jnp.concatenate([got_t[:, boxes:], -got_t[:, :boxes]], 1)
    out_ref[...] = jnp.dot(work[...].T.astype(BF16), rad[...], preferred_element_type=F32)
    all_of(list_got, list_got, list_ss, list_rs).wait_send()
    all_of(x_send, x_got, x_ss, x_rs.at[0]).wait_send()
    all_of(r_send, r_got, r_ss, r_rs).wait_send()
    for c in range(CHUNKS):
        pltpu.make_async_remote_copy(
            src_ref=x_all.at[c, pl.ds(0, n_narrow - 1)],
            dst_ref=x_all.at[c, pl.ds(0, n_narrow - 1)],
            send_sem=n_ss, recv_sem=n_rs.at[0], device_id=(me_w, n_up), device_id_type=MESH,
        ).wait_send()


def solution(mesh):
    n_wide, n_narrow = mesh.shape["wide"], mesh.shape["narrow"]
    n_z = 8
    both = ("wide", "narrow")

    def on_device(coef, rad, interp, angles, table, sources, operators, counts):
        boxes, _, n_bases = coef.shape
        q0, q1 = interp.shape
        n_ops = table.shape[0]
        n_list = sources.shape[1]
        chunk = 256
        parts = q1 // chunk
        rows = 2 * n_wide
        rad_raw = jnp.transpose(rad, (2, 0, 1))
        table_t = jnp.transpose(table, (1, 2, 0))
        n_tab = -(-n_ops // LANES) * LANES
        assert n_list <= GROUP * STEPS
        vmem = pl.BlockSpec(memory_space=pltpu.VMEM)
        anyw = pl.BlockSpec(memory_space=pl.ANY)
        dma = pltpu.SemaphoreType.DMA
        slots = (n_wide, 2, 2 * LANES)
        result = pl.pallas_call(
            functools.partial(kernel, (n_wide, n_narrow, n_z, chunk)),
            out_shape=jax.ShapeDtypeStruct((2 * boxes, n_bases), F32),
            in_specs=[anyw] * 8,
            out_specs=vmem,
            scratch_shapes=[
                pltpu.SMEM(counts.shape, jnp.int32),
                pltpu.VMEM(coef.shape, BF16),
                pltpu.VMEM(angles.shape, F32),
                pltpu.VMEM(table_t.shape, F32),
                pltpu.VMEM(sources.shape, jnp.int32),
                pltpu.VMEM(operators.shape, jnp.int32),
                pltpu.VMEM((q0, 2, n_bases), BF16),
                pltpu.VMEM((2 * q0, n_bases), BF16),
                pltpu.VMEM((q0, q1), BF16),
                pltpu.VMEM((8, q1), F32),
                pltpu.VMEM((8, q1), F32),
                pltpu.VMEM((2 * q0, 2 * boxes), F32),
                pltpu.VMEM((n_bases // LANES, 2 * boxes, LANES), F32),
                pltpu.VMEM((4, q1), F32),
                pltpu.VMEM((2, 2 * LANES), jnp.int32),
                pltpu.VMEM(slots, jnp.int32),
                pltpu.VMEM((SHARES * STEPS, rows // SHARES, LANES), jnp.int32),
                pltpu.VMEM(slots, F32),
                pltpu.VMEM(slots, F32),
                pltpu.VMEM((CHUNKS, n_narrow, rows // CHUNKS, 2 * LANES), F32),
                pltpu.VMEM((n_tab, 2 * LANES), BF16),
                pltpu.VMEM((SHARES * STEPS, GROUP * rows // SHARES, 2 * LANES), BF16),
                pltpu.VMEM((2 * boxes, q1), BF16),
                pltpu.VMEM(slots, F32),
                pltpu.VMEM(slots, F32),
                pltpu.VMEM((4, q1), F32),
                pltpu.VMEM((q0, 2 * boxes), F32),
                dma((parts + 7,)),
                dma, dma, dma, dma((CHUNKS,)), dma, dma((CHUNKS * n_narrow,)), dma, dma,
            ],
            compiler_params=pltpu.CompilerParams(
                collective_id=0, has_side_effects=True, vmem_limit_bytes=60 * 1024 * 1024
            ),
            name="fmm_step",
        )(counts, coef, rad_raw, interp, angles, table_t, sources, operators)
        return jnp.transpose(result.reshape(2, boxes, n_bases), (1, 0, 2))

    return jax.shard_map(
        on_device,
        mesh=mesh,
        in_specs=(
            P(both, None, None), P(), P(), P(), P(None, None, "wide"),
            P(both, None), P(both, None), P(both),
        ),
        out_specs=P(both, None, None),
        check_vma=False,
    )
```

time: 46.2 us -> 40.5 us (0.88)
  Pallas kernels: 44.6 us -> 38.8 us
    pallas_call x1, Pallas kernels: 44.6 us -> 38.8 us  [on_device(): pl.pallas_call(functools.partial(kernel, (n_wide, n_narrow, n_z, chunk)),...]
    reshape x0 -> x1, local copies, waits for them, and re-layouts: none -> 1.52 us  [on_device(): return jnp.transpose(result.reshape(2, boxes, n_bases), (1, 0, 2))]
    unnamed x1 -> x0, local copies, waits for them, and re-layouts: 1.47 us -> none
where the time goes in v3:
time: 40.5 us; the launch traced here: 40.3 us
  Pallas kernels  38.8 us (96%)
  local copies, waits for them, and re-layouts  1.52 us (4%)
    pallas_call x1, Pallas kernels, on_device(): pl.pallas_call(functools.partial(kernel, (n_wide, n_narrow, n_z, chunk)),...  38.8 us
    reshape x1, local copies, waits for them, and re-layouts, on_device(): return jnp.transpose(result.reshape(2, boxes, n_bases), (1, 0, 2))  1.52 us

profile of v3, /device:TPU:1, one launch (start us, length us, event | category | flops | bytes accessed | tf_op | source)
XLA Modules:
  0.0 40.3 jit_solution(11735509194403624003)
XLA Ops:
  0.0 38.8 %fmm_step.1 = f32[32,512]{1,0:T(8,128)} custom-call(s32[2]{0:T(128)} %counts_hbm.1, bf16[16,2,512]{2,1,0:T(2,128)(2,1)} %coef_hbm.1, bf16[882,2,512]{2,1,0:T(2,128)(2,1)} %bitcast.6, bf16[882,3328]{1,0:T(8,128)(2,1)} %int_hbm.1, f32[8,3328]{1,0:T(8,128)} %ang_hbm.1, f32[2,104,316]{2,1,0:T(8,128)} %bitcast.7, s32[2,189]{1,0:T(2,128)} %src_hbm.1, s32[2,189]{1,0:T(2,128)} %opr_hbm.1), custom_call_target="tpu_custom_call" | custom-call | tf_op jit(solution)/shard_map/fmm_step/pallas_call | solution.py:364
  38.8 1.5 %copy.11 = f32[2,16,512]{2,0,1:T(2,128)} copy(f32[2,16,512]{2,1,0:T(8,128)} %bitcast.8) | data formatting | bytes 131072 | tf_op jit(solution)/shard_map/reshape | solution.py:405

commit v4 on v3

--- a/solution.py
+++ b/solution.py
@@ -15,6 +15,8 @@
 STEPS = 2
 SHARES = 4
 CHUNKS = 2
+ROWS = 112
+FIELDS = 3
 NO_OPERATOR = 511
 
 
@@ -30,8 +32,8 @@
     counts_hbm, coef_hbm, rad_hbm, int_hbm, ang_hbm, tab_hbm, src_hbm, opr_hbm,
     out_ref,
     counts_ref, coef_ref, ang_ref, tab_ref, src_ref, opr_ref,
-    raw, rad, itp, cosv, sinv, work, coefs, outg, list_send, list_got, lists, x_send, x_got, x_all,
-    tab, picks, down, r_send, r_got, inc, recv_acc,
+    raw, rad, itp, cosv, sinv, work, planes, coefs, outg, list_send, list_got, lists, x_send, x_got, x_all,
+    tab, picks, down, r_send, r_got, inc,
     mem_sem, list_ss, list_rs, x_ss, x_rs, n_ss, n_rs, r_ss, r_rs,
 ):
     n_wide, n_narrow, n_z, chunk = dims
@@ -49,24 +51,24 @@
     boxes = coef_ref.shape[0]
 
     small = [
-        pltpu.make_async_copy(a, b, mem_sem.at[parts + 1 + i])
+        pltpu.make_async_copy(a, b, mem_sem.at[parts + i])
         for i, (a, b) in enumerate([
-            (ang_hbm, ang_ref), (coef_hbm, coef_ref), (src_hbm, src_ref), (opr_hbm, opr_ref),
-            (counts_hbm, counts_ref), (tab_hbm, tab_ref),
+            (coef_hbm, coef_ref), (src_hbm, src_ref), (opr_hbm, opr_ref),
+            (counts_hbm, counts_ref), (ang_hbm, ang_ref), (tab_hbm, tab_ref),
         ])
     ]
     small[0].start()
-    rad_copy = pltpu.make_async_copy(rad_hbm, raw, mem_sem.at[parts])
-    rad_copy.start()
-    for copy in small[1:]:
+    blocks = [(q, min(q + ROWS, q0)) for q in range(0, q0, ROWS)]
+    rad_copies = [
+        pltpu.make_async_copy(rad_hbm.at[a:b], raw.at[a:b], mem_sem.at[parts + 6 + i])
+        for i, (a, b) in enumerate(blocks)
+    ]
+    for copy in rad_copies + small[1:5]:
         copy.start()
 
     def int_copy(i):
         cols = pl.ds(i * chunk, chunk)
         return pltpu.make_async_copy(int_hbm.at[:, cols], itp.at[:, cols], mem_sem.at[i])
-
-    for i in range(parts):
-        int_copy(i).start()
 
     barrier = pltpu.get_barrier_semaphore()
     offsets = offsets_along(n_x, n_z)
@@ -88,13 +90,65 @@
     for n in (n_up, n_dn, n_par, n_cross):
         pl.semaphore_signal(barrier, 1, device_id=(me_w, n), device_id_type=MESH)
 
+    for i in range(parts):
+        int_copy(i).start()
+    small[5].start()
+
     small[0].wait()
-    for i in range(parts):
+    tiled = coef_ref[...].astype(F32).reshape(2 * boxes, -1)
+    bases = range(coefs.shape[0])
+    for t in bases:
+        coefs[t] = tiled[:, t * LANES : (t + 1) * LANES]
+    real, imag = [
+        jnp.concatenate([coefs[t, pl.ds(c, boxes, stride=2), :] for t in bases], 1)
+        for c in range(2)
+    ]
+    coef = jnp.concatenate(
+        [jnp.concatenate([real, -imag], 1), jnp.concatenate([imag, real], 1)], 0
+    ).astype(BF16)
+
+    n_bases = rad_hbm.shape[2]
+    for copy, (a, b) in zip(rad_copies, blocks):
+        copy.wait()
+        rows = pl.ds(2 * a, 2 * (b - a))
+        rad[rows, :] = raw[a:b].reshape(2 * (b - a), n_bases)
+        for t in bases:
+            work[t, rows, :] = rad[rows, pl.ds(t * LANES, LANES)].astype(F32)
+            for c in range(2):
+                planes[pl.ds(a, b - a), pl.ds(c * n_bases + t * LANES, LANES)] = work[
+                    t, pl.ds(2 * a + c, b - a, stride=2), :
+                ].astype(BF16)
+    leaf = lax.dot_general(
+        coef, planes[...], (((1,), (1,)), ((), ())), preferred_element_type=F32
+    ).astype(BF16)
+
+    def up_chunk(i):
         cols = pl.ds(i * chunk, chunk)
-        cosv[:, cols] = jnp.cos(ang_ref[:, cols])
-        sinv[:, cols] = jnp.sin(ang_ref[:, cols])
-
-    for copy in small[1:]:
+        ang = ang_ref[:, cols]
+        co = jnp.cos(ang)
+        si = jnp.sin(ang)
+        cosv[:, cols] = co
+        sinv[:, cols] = si
+        up = jnp.dot(leaf, itp[:, cols], preferred_element_type=F32)
+        for p in range(2):
+            ur = up[8 * p : 8 * p + 8]
+            ui = up[boxes + 8 * p : boxes + 8 * p + 8]
+            outg[pl.ds(p, 1), cols] = jnp.sum(co * ur - si * ui, 0, keepdims=True)
+            outg[pl.ds(2 + p, 1), cols] = jnp.sum(co * ui + si * ur, 0, keepdims=True)
+
+    small[4].wait()
+    groups = [(0, 4), (4, 8), (8, 11), (11, parts)]
+
+    def up_group(first, last):
+        for i in range(first, last):
+            int_copy(i).wait()
+        for i in range(first, last):
+            up_chunk(i)
+
+    for g in groups[:-1]:
+        up_group(*g)
+
+    for copy in small[1:4]:
         copy.wait()
     src = src_ref[...]
     opr = opr_ref[...]
@@ -103,71 +157,21 @@
     lane = lax.broadcasted_iota(jnp.int32, src.shape, 1)
     which = lax.broadcasted_iota(jnp.int32, src.shape, 0)
     limit = jnp.where(which == 0, counts_ref[0], counts_ref[1])
-    packed = row * 512 + jnp.where(lane < limit, opr, NO_OPERATOR)
-    list_send[...] = jnp.full(list_send.shape, NO_OPERATOR, jnp.int32)
-    list_send[:, pl.ds(0, GROUP)] = packed[:, :GROUP]
-    list_send[:, pl.ds(LANES, n_list - GROUP)] = packed[:, GROUP:]
-
-    n_ops = tab_ref.shape[2]
-    for c in range(2):
-        t = tab_ref[c]
-        t = jnp.concatenate([t, jnp.zeros((LANES - dirs, n_ops), F32)], 0)
-        t = jnp.concatenate([t, jnp.zeros((LANES, tab.shape[0] - n_ops), F32)], 1)
-        tab[:, pl.ds(c * LANES, LANES)] = t.T.astype(BF16)
-
-    tiled = coef_ref[...].astype(F32).reshape(2 * boxes, -1)
-    bases = range(coefs.shape[0])
-    for t in bases:
-        coefs[t] = tiled[:, t * LANES : (t + 1) * LANES]
-    coef = jnp.concatenate(
-        [
-            jnp.concatenate([coefs[t, pl.ds(c, boxes, stride=2), :] for t in bases], 1)
-            for c in range(2)
-        ],
-        0,
-    ).astype(BF16)
-
-    rad_copy.wait()
-    rad[...] = raw[...].reshape(rad.shape)
-    work[...] = lax.dot_general(
-        rad[...], coef, (((1,), (1,)), ((), ())), preferred_element_type=F32
-    )
-    by_real = work[pl.ds(0, q0, stride=2), :]
-    by_imag = work[pl.ds(1, q0, stride=2), :]
-    leaf_t = jnp.concatenate(
-        [by_real[:, :boxes] - by_imag[:, boxes:], by_imag[:, :boxes] + by_real[:, boxes:]], 1
-    )
-    leaf = leaf_t.T.astype(BF16)
-
-    def up_chunk(i):
-        cols = pl.ds(i * chunk, chunk)
-        co = cosv[:, cols]
-        si = sinv[:, cols]
-        int_copy(i).wait()
-        up = jnp.dot(leaf, itp[:, cols], preferred_element_type=F32)
-        for p in range(2):
-            ur = up[8 * p : 8 * p + 8]
-            ui = up[boxes + 8 * p : boxes + 8 * p + 8]
-            outg[pl.ds(p, 1), cols] = jnp.sum(co * ur - si * ui, 0, keepdims=True)
-            outg[pl.ds(2 + p, 1), cols] = jnp.sum(co * ui + si * ur, 0, keepdims=True)
-
-    early = parts * 3 // 4
-    for i in range(early):
-        up_chunk(i)
-
-    pl.semaphore_wait(barrier, n_wide - 1 + 4)
-
-    def list_copy(w, there):
-        return pltpu.make_async_remote_copy(
-            src_ref=list_send, dst_ref=list_got.at[there], send_sem=list_ss, recv_sem=list_rs,
-            device_id=(w, me_n), device_id_type=MESH)
-
-    for w, there in peers[:-1]:
-        list_copy(w, there).start()
-    list_got[n_wide - 1] = list_send[...]
-
-    for i in range(early, parts):
-        up_chunk(i)
+    wanted = jnp.where(lane < limit, opr, NO_OPERATOR)
+    n_words = n_list // FIELDS
+    at = lax.broadcasted_iota(jnp.int32, (1, LANES), 1)
+    for kind, value in enumerate((wanted, row)):
+        value = jnp.concatenate(
+            [value, jnp.full((2, 2 * LANES - n_list), NO_OPERATOR, jnp.int32)], 1
+        )
+        word = jnp.zeros((2, LANES), jnp.int32)
+        for k in range(FIELDS):
+            word = word + (pltpu.roll(value, (2 * LANES - k * n_words) % (2 * LANES), 1)[:, :LANES] << (9 * k))
+        list_send[pl.ds(kind, 1), :] = jnp.where(
+            at < LANES // 2, word[0:1], pltpu.roll(word[1:2], LANES // 2, 1)
+        )
+
+    up_group(*groups[-1])
 
     for w in range(n_wide):
         tile, off = divmod(w * dirs, LANES)
@@ -192,9 +196,28 @@
             src_ref=src_all.at[some], dst_ref=dst_all.at[some], send_sem=send_sem,
             recv_sem=recv_sem, device_id=(peers[0][0], me_n), device_id_type=MESH)
 
+    pl.semaphore_wait(barrier, n_wide - 1 + 4)
     for w, there in peers[:-1]:
         slice_copy(x_send, w, x_got, there, w, x_ss, x_rs.at[there // per_chunk]).start()
     x_got[n_wide - 1] = x_send[me_w]
+
+    def list_copy(w, there):
+        return pltpu.make_async_remote_copy(
+            src_ref=list_send, dst_ref=list_got.at[there], send_sem=list_ss, recv_sem=list_rs,
+            device_id=(w, me_n), device_id_type=MESH)
+
+    for w, there in peers[:-1]:
+        list_copy(w, there).start()
+    list_got[n_wide - 1] = list_send[...]
+
+
+    small[5].wait()
+    n_ops = tab_ref.shape[2]
+    for c in range(2):
+        t = tab_ref[c]
+        t = jnp.concatenate([t, jnp.zeros((LANES - dirs, n_ops), F32)], 0)
+        t = jnp.concatenate([t, jnp.zeros((LANES, tab.shape[0] - n_ops), F32)], 1)
+        tab[:, pl.ds(c * LANES, LANES)] = t.T.astype(BF16)
 
     lane_at = lax.broadcasted_iota(jnp.int32, (GROUP * per_share, LANES), 1)
     rows_all = n_narrow * n_rows
@@ -210,16 +233,8 @@
         for t in range(0, rows_all, LANES)
     ]
 
-    all_of(list_got, list_got, list_ss, list_rs).wait_recv()
-    for h in range(SHARES):
-        mine = slice(h * n_wide // SHARES, (h + 1) * n_wide // SHARES)
-        for t in range(STEPS):
-            lists[h * STEPS + t] = list_got[mine, :, t * LANES : (t + 1) * LANES].reshape(
-                per_share, LANES
-            )
-
-    def entries(g):
-        here = lists[g]
+    def entries(g, kind):
+        here = lists[kind, g]
         columns = [here[:, u : u + 1] for u in range(GROUP)]
         return jnp.concatenate([jnp.broadcast_to(c, (per_share, LANES)) for c in columns], 0)
 
@@ -230,8 +245,8 @@
     operators_at = [lane_at + t for t in range(0, tab.shape[0], LANES)]
 
     def pick_operators(g, c):
-        onehot = one_hot(entries(g) & 511, operators_at)
-        picks[g] = jnp.dot(onehot, tab[...], preferred_element_type=F32).astype(BF16)
+        onehot = one_hot(entries(g, 0), operators_at)
+        picks[g] = jnp.dot(onehot, tab[...], preferred_element_type=F32)
         return c
 
     def pick(first, last):
@@ -257,24 +272,34 @@
         block_copy(c, n_up, n_up).wait_recv()
         block_copy(c, n_up, n_par).start()
 
-    pick(0, 1)
     gather_slices(1)
-    pick(1, 2)
     gather_slices(0)
-    pick(2, 3)
+    all_of(list_got, list_got, list_ss, list_rs).wait_recv()
+    first = GROUP - n_words
+    lane = lax.broadcasted_iota(jnp.int32, (per_share, LANES), 1)
+    for h in range(SHARES):
+        mine = slice(h * n_wide // SHARES, (h + 1) * n_wide // SHARES)
+        for kind in range(2):
+            words = list_got[mine, kind, :]
+            words = jnp.concatenate([words, pltpu.roll(words, LANES // 2, 1)], 0)
+            field = [lax.shift_right_logical(words, 9 * k) & 511 for k in range(FIELDS)]
+            early = jnp.where(lane < n_words, field[0], pltpu.roll(field[1], n_words, 1))
+            late = jnp.where(lane < n_words, field[2], pltpu.roll(field[1], n_words - first, 1))
+            lists[kind, h * STEPS] = early
+            lists[kind, h * STEPS + 1] = jnp.where(lane < n_list - GROUP, late, NO_OPERATOR)
     pass_on(1)
-    pick(3, 5)
+    pick(0, 2)
     pass_on(0)
-    pick(5, SHARES * STEPS)
+    pick(2, SHARES * STEPS)
     for c in range(CHUNKS):
         for n in (n_far, n_par, n_par + n_up - me_n, n_par + n_dn - me_n, n_par + n_far - me_n):
             block_copy(c, n, n_up).wait_recv()
     pat = x_all[...].astype(BF16).reshape(rows_all, 2 * LANES)
 
     def translate(g, c):
-        onehot = one_hot(lax.shift_right_logical(entries(g), 9), row_at)
+        onehot = one_hot(entries(g, 1), row_at)
         px = jnp.dot(onehot, pat, preferred_element_type=F32)
-        pt = picks[g].astype(F32)
+        pt = picks[g]
         xr, xi = px[:, :LANES], px[:, LANES:]
         tr, ti = pt[:, :LANES], pt[:, LANES:]
         real = (tr * xr - ti * xi).reshape(GROUP, per_share, LANES).sum(0)
@@ -285,8 +310,10 @@
         zero = jnp.zeros((per_share, LANES), F32)
         real, imag = lax.fori_loop(h * STEPS, (h + 1) * STEPS, translate, (zero, zero))
         mine = slice(h * n_wide // SHARES, (h + 1) * n_wide // SHARES)
-        r_send[mine, :, pl.ds(0, LANES)] = real.reshape(-1, 2, LANES)
-        r_send[mine, :, pl.ds(LANES, LANES)] = imag.reshape(-1, 2, LANES)
+        for j in range(2):
+            rows = slice(j * per_share // 2, (j + 1) * per_share // 2)
+            r_send[mine, j, pl.ds(0, LANES)] = real[rows]
+            r_send[mine, j, pl.ds(LANES, LANES)] = imag[rows]
         for i in range(mine.start, min(mine.stop, n_wide - 1)):
             slice_copy(r_send, i, r_got, me_w, peers[i][0], r_ss, r_rs).start()
     r_got[me_w] = r_send[n_wide - 1]
@@ -321,14 +348,15 @@
             real.append(co * ir + si * ii)
             imag.append(co * ii - si * ir)
         down[:, cols] = jnp.concatenate(real + imag, 0).astype(BF16)
-    recv_acc[...] = lax.dot_general(
-        itp[...], down[...], (((1,), (1,)), ((), ())), preferred_element_type=F32
-    )
-
-    got_t = recv_acc[...]
-    work[pl.ds(0, q0, stride=2), :] = got_t
-    work[pl.ds(1, q0, stride=2), :] = jnp.concatenate([got_t[:, boxes:], -got_t[:, :boxes]], 1)
-    out_ref[...] = jnp.dot(work[...].T.astype(BF16), rad[...], preferred_element_type=F32)
+    received = lax.dot_general(
+        down[...], itp[...], (((1,), (1,)), ((), ())), preferred_element_type=F32
+    ).astype(BF16)
+
+    both = jnp.dot(received, planes[...], preferred_element_type=F32)
+    by_real, by_imag = both[:, :n_bases], both[:, n_bases:]
+    out_ref[pl.ds(0, boxes), :] = by_real[:boxes] + by_imag[boxes:]
+    out_ref[pl.ds(boxes, boxes), :] = by_real[boxes:] - by_imag[:boxes]
+
     all_of(list_got, list_got, list_ss, list_rs).wait_send()
     all_of(x_send, x_got, x_ss, x_rs.at[0]).wait_send()
     all_of(r_send, r_got, r_ss, r_rs).wait_send()
@@ -356,7 +384,8 @@
         rad_raw = jnp.transpose(rad, (2, 0, 1))
         table_t = jnp.transpose(table, (1, 2, 0))
         n_tab = -(-n_ops // LANES) * LANES
-        assert n_list <= GROUP * STEPS
+        assert n_list % FIELDS == 0 and n_list <= GROUP * STEPS
+        assert n_list // FIELDS <= LANES // 2
         vmem = pl.BlockSpec(memory_space=pltpu.VMEM)
         anyw = pl.BlockSpec(memory_space=pl.ANY)
         dma = pltpu.SemaphoreType.DMA
@@ -378,23 +407,23 @@
                 pltpu.VMEM((q0, q1), BF16),
                 pltpu.VMEM((8, q1), F32),
                 pltpu.VMEM((8, q1), F32),
-                pltpu.VMEM((2 * q0, 2 * boxes), F32),
+                pltpu.VMEM((n_bases // LANES, 2 * q0, LANES), F32),
+                pltpu.VMEM((q0, 2 * n_bases), BF16),
                 pltpu.VMEM((n_bases // LANES, 2 * boxes, LANES), F32),
                 pltpu.VMEM((4, q1), F32),
-                pltpu.VMEM((2, 2 * LANES), jnp.int32),
-                pltpu.VMEM(slots, jnp.int32),
-                pltpu.VMEM((SHARES * STEPS, rows // SHARES, LANES), jnp.int32),
+                pltpu.VMEM((2, LANES), jnp.int32),
+                pltpu.VMEM((n_wide, 2, LANES), jnp.int32),
+                pltpu.VMEM((2, SHARES * STEPS, rows // SHARES, LANES), jnp.int32),
                 pltpu.VMEM(slots, F32),
                 pltpu.VMEM(slots, F32),
                 pltpu.VMEM((CHUNKS, n_narrow, rows // CHUNKS, 2 * LANES), F32),
                 pltpu.VMEM((n_tab, 2 * LANES), BF16),
-                pltpu.VMEM((SHARES * STEPS, GROUP * rows // SHARES, 2 * LANES), BF16),
+                pltpu.VMEM((SHARES * STEPS, GROUP * rows // SHARES, 2 * LANES), F32),
                 pltpu.VMEM((2 * boxes, q1), BF16),
                 pltpu.VMEM(slots, F32),
                 pltpu.VMEM(slots, F32),
                 pltpu.VMEM((4, q1), F32),
-                pltpu.VMEM((q0, 2 * boxes), F32),
-                dma((parts + 7,)),
+                dma((parts + 6 + -(-q0 // ROWS),)),
                 dma, dma, dma, dma((CHUNKS,)), dma, dma((CHUNKS * n_narrow,)), dma, dma,
             ],
             compiler_params=pltpu.CompilerParams(

time: 40.5 us -> 37.7 us (0.931)
  Pallas kernels: 38.8 us -> 35.8 us
    pallas_call x1, Pallas kernels: 38.8 us -> 35.8 us  [on_device(): pl.pallas_call(functools.partial(kernel, (n_wide, n_narrow, n_z, chunk)),...]
where the time goes in v4:
time: 37.7 us; the launch traced here: 37.4 us
  Pallas kernels  35.8 us (95%)
  local copies, waits for them, and re-layouts  1.52 us (4%)
    pallas_call x1, Pallas kernels, on_device(): pl.pallas_call(functools.partial(kernel, (n_wide, n_narrow, n_z, chunk)),...  35.8 us
    reshape x1, local copies, waits for them, and re-layouts, on_device(): return jnp.transpose(result.reshape(2, boxes, n_bases), (1, 0, 2))  1.52 us

profile of v4, /device:TPU:1, one launch (start us, length us, event | category | flops | bytes accessed | tf_op | source)
XLA Modules:
  0.0 37.4 jit_solution(16049301964337469385)
XLA Ops:
  0.0 35.8 %fmm_step.1 = f32[32,512]{1,0:T(8,128)} custom-call(s32[2]{0:T(128)} %counts_hbm.1, bf16[16,2,512]{2,1,0:T(2,128)(2,1)} %coef_hbm.1, bf16[882,2,512]{2,1,0:T(2,128)(2,1)} %bitcast.6, bf16[882,3328]{1,0:T(8,128)(2,1)} %int_hbm.1, f32[8,3328]{1,0:T(8,128)} %ang_hbm.1, f32[2,104,316]{2,1,0:T(8,128)} %bitcast.7, s32[2,189]{1,0:T(2,128)} %src_hbm.1, s32[2,189]{1,0:T(2,128)} %opr_hbm.1), custom_call_target="tpu_custom_call" | custom-call | tf_op jit(solution)/shard_map/fmm_step/pallas_call | solution.py:393
  35.9 1.5 %copy.11 = f32[2,16,512]{2,0,1:T(2,128)} copy(f32[2,16,512]{2,1,0:T(8,128)} %bitcast.8) | data formatting | bytes 131072 | tf_op jit(solution)/shard_map/reshape | solution.py:434

commit v5 on v4

--- a/solution.py
+++ b/solution.py
@@ -392,7 +392,7 @@
         slots = (n_wide, 2, 2 * LANES)
         result = pl.pallas_call(
             functools.partial(kernel, (n_wide, n_narrow, n_z, chunk)),
-            out_shape=jax.ShapeDtypeStruct((2 * boxes, n_bases), F32),
+            out_shape=pltpu.VMEM((2 * boxes, n_bases), F32),
             in_specs=[anyw] * 8,
             out_specs=vmem,
             scratch_shapes=[

time: 37.7 us -> 36.2 us (0.960)
  local copies, waits for them, and re-layouts: 1.52 us -> 0.68 us
  Pallas kernels: 35.8 us -> 35.2 us
    reshape x1, local copies, waits for them, and re-layouts: 1.52 us -> 0.68 us  [on_device(): return jnp.transpose(result.reshape(2, boxes, n_bases), (1, 0, 2))]
    pallas_call x1, Pallas kernels: 35.8 us -> 35.2 us  [on_device(): pl.pallas_call(functools.partial(kernel, (n_wide, n_narrow, n_z, chunk)),...]
where the time goes in v5:
time: 36.2 us; the launch traced here: 35.9 us
  Pallas kernels  35.2 us (97%)
  local copies, waits for them, and re-layouts  0.68 us (2%)
    pallas_call x1, Pallas kernels, on_device(): pl.pallas_call(functools.partial(kernel, (n_wide, n_narrow, n_z, chunk)),...  35.2 us

profile of v5, /device:TPU:1, one launch (start us, length us, event | category | flops | bytes accessed | tf_op | source)
XLA Modules:
  0.0 35.9 jit_solution(8262230862203248662)
XLA Ops:
  0.0 35.2 %fmm_step.1 = f32[32,512]{1,0:T(8,128)S(1)} custom-call(s32[2]{0:T(128)} %counts_hbm.1, bf16[16,2,512]{2,1,0:T(2,128)(2,1)} %coef_hbm.1, bf16[882,2,512]{2,1,0:T(2,128)(2,1)} %bitcast.7, bf16[882,3328]{1,0:T(8,128)(2,1)} %int_hbm.1, f32[8,3328]{1,0:T(8,128)} %ang_hbm.1, f32[2,104,316]{2,1,0:T(8,128)} %bitcast.8, s32[2,189]{1,0:T(2,128)} %src_hbm.1, ...), custom_call_target="tpu_custom_call" | custom-call | tf_op jit(solution)/shard_map/fmm_step/pallas_call | solution.py:393
  35.2 0.7 %copy.11 = f32[2,16,512]{2,0,1:T(2,128)} copy(f32[2,16,512]{2,1,0:T(8,128)S(1)} %bitcast.6) | data formatting | bytes 131072 | tf_op jit(solution)/shard_map/reshape | solution.py:434

commit v6 on v5

--- a/solution.py
+++ b/solution.py
@@ -14,7 +14,7 @@
 GROUP = 96
 STEPS = 2
 SHARES = 4
-CHUNKS = 2
+NEAR_FROM = 20
 ROWS = 112
 FIELDS = 3
 NO_OPERATOR = 511
@@ -47,7 +47,7 @@
     n_list = src_ref.shape[1]
     n_rows = 2 * n_wide
     per_share = n_rows // SHARES
-    per_chunk = n_wide // CHUNKS
+    spans = [(0, NEAR_FROM), (NEAR_FROM, n_wide)]
     boxes = coef_ref.shape[0]
 
     small = [
@@ -198,7 +198,7 @@
 
     pl.semaphore_wait(barrier, n_wide - 1 + 4)
     for w, there in peers[:-1]:
-        slice_copy(x_send, w, x_got, there, w, x_ss, x_rs.at[there // per_chunk]).start()
+        slice_copy(x_send, w, x_got, there, w, x_ss, x_rs.at[int(there >= NEAR_FROM)]).start()
     x_got[n_wide - 1] = x_send[me_w]
 
     def list_copy(w, there):
@@ -222,12 +222,11 @@
     lane_at = lax.broadcasted_iota(jnp.int32, (GROUP * per_share, LANES), 1)
     rows_all = n_narrow * n_rows
     spot = lax.broadcasted_iota(jnp.int32, (8, rows_all), 1)
-    per_part = 2 * per_chunk
-    place_of = (spot // (n_narrow * per_part)) * per_chunk + spot % per_part // 2
+    place_of = spot % n_rows // 2
     holds = jnp.zeros((8, rows_all), jnp.int32)
     for i, (w, _) in enumerate(peers):
         holds = jnp.where(place_of == i, w, holds)
-    holds = spot // per_part % n_narrow * n_rows + holds * 2 + spot % 2
+    holds = spot // n_rows * n_rows + holds * 2 + spot % 2
     row_at = [
         jnp.broadcast_to(holds[0:1, t : t + LANES], (GROUP * per_share, LANES))
         for t in range(0, rows_all, LANES)
@@ -252,16 +251,20 @@
     def pick(first, last):
         lax.fori_loop(first, last, pick_operators, 0)
 
+    def rows_of(c):
+        first, last = spans[c]
+        return pl.ds(2 * first, 2 * (last - first))
+
     def block_copy(c, block, to):
         return pltpu.make_async_remote_copy(
-            src_ref=x_all.at[c, block], dst_ref=x_all.at[c, block], send_sem=n_ss,
+            src_ref=x_all.at[block, rows_of(c)], dst_ref=x_all.at[block, rows_of(c)], send_sem=n_ss,
             recv_sem=n_rs.at[c * n_narrow + block], device_id=(me_w, to), device_id_type=MESH)
 
     def gather_slices(c):
-        first = c * per_chunk
-        count = per_chunk if c == 0 else per_chunk - 1
+        first, last = spans[c]
+        count = min(last, n_wide - 1) - first
         all_of(x_got, x_got, x_ss, x_rs.at[c], first, count).wait_recv()
-        x_all[c, me_n] = x_got[first : first + per_chunk].reshape(per_part, 2 * LANES)
+        x_all[me_n, rows_of(c), :] = x_got[first:last].reshape(2 * (last - first), 2 * LANES)
         for to in (n_up, n_dn, n_par):
             block_copy(c, me_n, to).start()
 
@@ -291,7 +294,7 @@
     pick(0, 2)
     pass_on(0)
     pick(2, SHARES * STEPS)
-    for c in range(CHUNKS):
+    for c in range(2):
         for n in (n_far, n_par, n_par + n_up - me_n, n_par + n_dn - me_n, n_par + n_far - me_n):
             block_copy(c, n, n_up).wait_recv()
     pat = x_all[...].astype(BF16).reshape(rows_all, 2 * LANES)
@@ -360,12 +363,11 @@
     all_of(list_got, list_got, list_ss, list_rs).wait_send()
     all_of(x_send, x_got, x_ss, x_rs.at[0]).wait_send()
     all_of(r_send, r_got, r_ss, r_rs).wait_send()
-    for c in range(CHUNKS):
-        pltpu.make_async_remote_copy(
-            src_ref=x_all.at[c, pl.ds(0, n_narrow - 1)],
-            dst_ref=x_all.at[c, pl.ds(0, n_narrow - 1)],
-            send_sem=n_ss, recv_sem=n_rs.at[0], device_id=(me_w, n_up), device_id_type=MESH,
-        ).wait_send()
+    blocks = pl.ds(0, n_narrow - 1)
+    pltpu.make_async_remote_copy(
+        src_ref=x_all.at[blocks], dst_ref=x_all.at[blocks], send_sem=n_ss, recv_sem=n_rs.at[0],
+        device_id=(me_w, n_up), device_id_type=MESH,
+    ).wait_send()
 
 
 def solution(mesh):
@@ -416,7 +418,7 @@
                 pltpu.VMEM((2, SHARES * STEPS, rows // SHARES, LANES), jnp.int32),
                 pltpu.VMEM(slots, F32),
                 pltpu.VMEM(slots, F32),
-                pltpu.VMEM((CHUNKS, n_narrow, rows // CHUNKS, 2 * LANES), F32),
+                pltpu.VMEM((n_narrow, rows, 2 * LANES), F32),
                 pltpu.VMEM((n_tab, 2 * LANES), BF16),
                 pltpu.VMEM((SHARES * STEPS, GROUP * rows // SHARES, 2 * LANES), F32),
                 pltpu.VMEM((2 * boxes, q1), BF16),
@@ -424,7 +426,7 @@
                 pltpu.VMEM(slots, F32),
                 pltpu.VMEM((4, q1), F32),
                 dma((parts + 6 + -(-q0 // ROWS),)),
-                dma, dma, dma, dma((CHUNKS,)), dma, dma((CHUNKS * n_narrow,)), dma, dma,
+                dma, dma, dma, dma((2,)), dma, dma((2 * n_narrow,)), dma, dma,
             ],
             compiler_params=pltpu.CompilerParams(
                 collective_id=0, has_side_effects=True, vmem_limit_bytes=60 * 1024 * 1024

time: 36.2 us -> 36 us (level)
  no operation moved by 1% of the time
where the time goes in v6:
time: 36 us; the launch traced here: 35.8 us
  Pallas kernels  35.1 us (98%)
  local copies, waits for them, and re-layouts  0.68 us (2%)
    pallas_call x1, Pallas kernels, on_device(): pl.pallas_call(functools.partial(kernel, (n_wide, n_narrow, n_z, chunk)),...  35.1 us

profile of v6, /device:TPU:1, one launch (start us, length us, event | category | flops | bytes accessed | tf_op | source)
XLA Modules:
  0.0 35.8 jit_solution(11419413781467258452)
XLA Ops:
  0.0 35.1 %fmm_step.1 = f32[32,512]{1,0:T(8,128)S(1)} custom-call(s32[2]{0:T(128)} %counts_hbm.1, bf16[16,2,512]{2,1,0:T(2,128)(2,1)} %coef_hbm.1, bf16[882,2,512]{2,1,0:T(2,128)(2,1)} %bitcast.7, bf16[882,3328]{1,0:T(8,128)(2,1)} %int_hbm.1, f32[8,3328]{1,0:T(8,128)} %ang_hbm.1, f32[2,104,316]{2,1,0:T(8,128)} %bitcast.8, s32[2,189]{1,0:T(2,128)} %src_hbm.1, ...), custom_call_target="tpu_custom_call" | custom-call | tf_op jit(solution)/shard_map/fmm_step/pallas_call | solution.py:395
  35.1 0.7 %copy.11 = f32[2,16,512]{2,0,1:T(2,128)} copy(f32[2,16,512]{2,1,0:T(8,128)S(1)} %bitcast.6) | data formatting | bytes 131072 | tf_op jit(solution)/shard_map/reshape | solution.py:436

commit v7 on v6

--- a/solution.py
+++ b/solution.py
@@ -249,7 +249,7 @@
         return c
 
     def pick(first, last):
-        lax.fori_loop(first, last, pick_operators, 0)
+        lax.fori_loop(first, last, pick_operators, 0, unroll=2 if last - first > 2 else 1)
 
     def rows_of(c):
         first, last = spans[c]

time: 36 us -> 35.9 us (level)
  no operation moved by 1% of the time
where the time goes in v7:
time: 35.9 us
  Pallas kernels  35.2 us (98%)
  local copies, waits for them, and re-layouts  0.68 us (2%)
    pallas_call x1, Pallas kernels, on_device(): pl.pallas_call(functools.partial(kernel, (n_wide, n_narrow, n_z, chunk)),...  35.2 us

profile of v7, /device:TPU:1, one launch (start us, length us, event | category | flops | bytes accessed | tf_op | source)
XLA Modules:
  0.0 35.9 jit_solution(5295337270733291969)
XLA Ops:
  0.0 35.2 %fmm_step.1 = f32[32,512]{1,0:T(8,128)S(1)} custom-call(s32[2]{0:T(128)} %counts_hbm.1, bf16[16,2,512]{2,1,0:T(2,128)(2,1)} %coef_hbm.1, bf16[882,2,512]{2,1,0:T(2,128)(2,1)} %bitcast.7, bf16[882,3328]{1,0:T(8,128)(2,1)} %int_hbm.1, f32[8,3328]{1,0:T(8,128)} %ang_hbm.1, f32[2,104,316]{2,1,0:T(8,128)} %bitcast.8, s32[2,189]{1,0:T(2,128)} %src_hbm.1, ...), custom_call_target="tpu_custom_call" | custom-call | tf_op jit(solution)/shard_map/fmm_step/pallas_call | solution.py:395
  35.2 0.7 %copy.11 = f32[2,16,512]{2,0,1:T(2,128)} copy(f32[2,16,512]{2,1,0:T(8,128)S(1)} %bitcast.6) | data formatting | bytes 131072 | tf_op jit(solution)/shard_map/reshape | solution.py:436
